TPU v7x, 32 devices: a whole 2x2x4 slice. The times are simulated.
32 devices in a mesh: dp: 16 (over z, x, core), head: 2 (over y).
Axes of the slice: x: 2, y: 2, z: 4, core: 2. Of those that a mesh axis runs over, the one named last changes fastest.
Arguments:
- tokens: bfloat16 [4, 8192, 768], P(None, 'dp'), may hold values from -6 to 6
- live: int32 [4, 8192], P(None, 'dp'), may hold values from 0 to 1, as said below
- bucket: int32 [4], replicated, may hold values from 64 to 512, as said below
- query_weight: bfloat16 [768, 768], P('dp', 'head'), may hold values from -0.21875 to 0.21875
- key_weight: bfloat16 [768, 768], P('dp', 'head'), may hold values from -0.21875 to 0.21875
- value_weight: bfloat16 [768, 768], P('dp', 'head'), may hold values from -0.21875 to 0.21875
- output_weight: bfloat16 [768, 768], P('head', 'dp'), may hold values from -0.875 to 0.875
- inner_weight: bfloat16 [768, 3072], P('dp', 'head'), may hold values from -0.21875 to 0.21875
- outer_weight: bfloat16 [3072, 768], P('head', 'dp'), may hold values from -0.109375 to 0.109375
- query_bias_vector: bfloat16 [768], P('head'), may hold values from -3 to 3
- value_bias_vector: bfloat16 [768], P('head'), may hold values from -3 to 3
- output_bias_vector: bfloat16 [768], replicated, may hold values from -3 to 3
- inner_bias_vector: bfloat16 [3072], P('head'), may hold values from -3 to 3
- outer_bias_vector: bfloat16 [768], replicated, may hold values from -3 to 3
- first_norm_scale: bfloat16 [768], replicated, may hold values from 0.099609375 to 1.8984375
- first_norm_bias: bfloat16 [768], replicated, may hold values from -2 to 2
- second_norm_scale: bfloat16 [768], replicated, may hold values from 0.099609375 to 1.8984375
- second_norm_bias: bfloat16 [768], replicated, may hold values from -2 to 2
- query_down_matrix: bfloat16 [768, 8], replicated, may hold values from -0.21875 to 0.21875
- value_down_matrix: bfloat16 [768, 8], replicated, may hold values from -0.21875 to 0.21875
- query_up_matrix: float32 [8, 768], P(None, 'head'), may hold values from -1.2 to 1.2
- value_up_matrix: float32 [8, 768], P(None, 'head'), may hold values from -1.2 to 1.2
- cotangent: bfloat16 [4, 8192, 768], P(None, 'dp'), may hold values from -6 to 6
Outputs:
- activations: bfloat16 [4, 8192, 768], P(None, 'dp')
- input_grad: bfloat16 [4, 8192, 768], P(None, 'dp')
- lora_query_grad: float32 [8, 768], P(None, 'head')
- lora_value_grad: float32 [8, 768], P(None, 'head')
Inputs may be any that keep to these rules, and one draw needn't show every extreme that they name: The four micro-batches take the bucket lengths 512, 256, 128 and 64, each once. The slots of micro-batch m form aligned items of bucket[m] slots; live is 1 on a prefix of each item longer than half of it and 0 after.
All inputs are finite; a program needn't handle non-finite values.
Results may differ from a plain program's by a relative error of at most 0.02.
Values may be sent and summed in bfloat16 or wider, within the bound.
No kernel may reach another device: no remote copies, remote signals or barrier semaphores. Data moves between devices by JAX's collectives and lax.ppermute only.
A program may use at most 192 MiB of HBM per device.

v0:
```python
import functools
import math

import jax
import jax.numpy as jnp
from jax import lax
from jax.experimental import pallas as pl
from jax.experimental.pallas import tpu as pltpu
from jax.sharding import PartitionSpec as P

F32, BF16 = jnp.float32, jnp.bfloat16
EPS = 1e-5
MASKED = -1e9
NT = (((1,), (1,)), ((), ()))
TN = (((0,), (0,)), ((), ()))
NN = (((1,), (0,)), ((), ()))
SWAP = [(0, 1), (1, 0)]
RSQRT2 = 1.0 / math.sqrt(2.0)
PHI0 = 1.0 / math.sqrt(2.0 * math.pi)
ONCE = pl.Buffered(1)
VMEM = 60 << 20


def work(flops):
    return pl.CostEstimate(flops=int(flops), bytes_accessed=8 << 20, transcendentals=0)


def chip_table(size, move):
    deep = size // 4

    def index(z, x, c, y):
        return ((z % deep) * 4 + x * 2 + c) * 2 + y

    return [
        (index(z, x, c, y), index(*move(z, x, c, y)))
        for z in range(deep)
        for x in range(2)
        for c in range(2)
        for y in range(2)
    ]


def by_permutes(size):
    return size == 16


def permuter(size):
    tables = {
        "first": chip_table(size, lambda z, x, c, y: (z, x, c, 1 - y) if c else (z, 1 - x, c, y)),
        "second": chip_table(size, lambda z, x, c, y: (z, 1 - x, c, y) if c else (z, x, c, 1 - y)),
        "ring": chip_table(size, lambda z, x, c, y: (z + 1, x, c, y)),
        "core": chip_table(size, lambda z, x, c, y: (z, x, 1 - c, y)),
    }
    return lambda a, which: lax.ppermute(a, ("dp", "head"), tables[which])


def then(value, done):
    return lax.optimization_barrier((value, done))[0]


def spread_ring(shard, size):
    go, blocks = permuter(size), [shard]
    for _ in range(3):
        blocks.append(go(blocks[-1], "ring"))
    return blocks


def gather_whole(shard):
    whole = lax.all_gather(shard, ("head", "dp"), axis=0, tiled=True)
    return [whole.reshape(2, -1, shard.shape[1])]


def sub_pieces(refs, info):
    dp, y = info[8], info[9]
    if len(refs) == 1:
        return [(refs[0].at[y ^ h], y ^ h, 0, h) for h in range(2)]
    rows = refs[0].shape[1]
    z, x, core = dp >> 2, (dp >> 1) & 1, dp & 1
    out = []
    for k in range(4):
        deep = ((z + 4 - k) & 3) << 2
        for side in range(2):
            c = core ^ side
            for j in range(4):
                dx, dy = ((0, 0), (1 - c, c), (c, 1 - c), (1, 1))[j]
                row = (deep + ((x ^ dx) << 1) + c) * rows
                view = refs[(k // 2) * 8 + side * 4 + j].at[k % 2]
                slot = dy * 16 + (k * 2 + side) * 2 + (1 if j in (1, 2) else 0)
                out.append((view, y ^ dy, pl.multiple_of(row, rows), slot))
    return out


def fetch(refs, info, parts, sems):
    subs = sub_pieces(refs, info)
    count = len(subs)
    result = []
    for p, (start, cols, dest) in enumerate(parts):
        copies = [
            pltpu.make_async_copy(
                ref.at[:, pl.ds(start, cols)], dest(h, row, ref.shape[0]), sems.at[p * count + slot]
            )
            for ref, h, row, slot in subs
        ]
        ref, h, row, _ = subs[0]
        waits = [
            pltpu.make_async_copy(
                ref.at[:, pl.ds(start, cols)], dest(h, row, ref.shape[0]), sems.at[p * count + slot]
            )
            for slot in range(count)
        ]
        result.append((copies, waits[: count // 2], waits[count // 2 :]))
    return result


def start_all(copies):
    for copy in copies:
        copy.start()


def wait_all(copies):
    for copy in copies:
        copy.wait()


def side_by_side(buf, count):
    return lambda h, row, rows: buf.at[pl.ds(row, rows), pl.ds(pl.multiple_of(h * count, 128), count)]


def stacked(buf):
    return lambda h, row, rows: buf.at[h, pl.ds(row, rows)]


def adapter_rows(own_ref, peer_ref, turn, rank):
    small = jnp.where(turn == 0, own_ref[: 2 * rank + 2], peer_ref[: 2 * rank + 2])
    uq, uv = split(2.0 * small[:rank]), split(2.0 * small[rank : 2 * rank])
    none = jnp.zeros((2 * rank, small.shape[1]), BF16)
    query = jnp.concatenate([uq[0], uq[1], none], axis=0)
    value = jnp.concatenate([none, uv[0], uv[1]], axis=0)
    rows = jnp.concatenate([query, jnp.zeros_like(query), value], axis=1)
    return rows, small[2 * rank : 2 * rank + 1], small[2 * rank + 1 : 2 * rank + 2]


def mm(a, b, dims=NN):
    return lax.dot_general(a, b, dims, preferred_element_type=F32)


def lane_masks():
    lane = lax.broadcasted_iota(jnp.int32, (1, 128), 1)
    one, zero = jnp.ones((1, 128), F32), jnp.zeros((1, 128), F32)
    low = jnp.where(lane < 64, one, zero)
    return low.astype(BF16), (one - low).astype(BF16)


def pack_kernel(*refs):
    out_ref, cols = refs[-1], refs[0].shape[1]
    for k, ref in enumerate(refs[:-1]):
        out_ref[:, k * cols : (k + 1) * cols] = ref[...]


def pack(parts):
    rows, cols = parts[0].shape
    return pl.pallas_call(
        pack_kernel,
        out_shape=jax.ShapeDtypeStruct((rows, len(parts) * cols), parts[0].dtype),
        name="pack",
    )(*parts)


def prepare_kernel(
    bucket, here, wo_ref, wi_ref, wt_ref, uq_ref, uv_ref, qb_ref, vb_ref, ib_ref,
    b0, b1, b2, b3, b4, b5, late_ref, small_ref, vec_ref, info_ref,
):
    half, hid = wo_ref.shape[0], wi_ref.shape[1]
    late_ref[:, :half] = wo_ref[...].T
    late_ref[:, half : half + hid] = wi_ref[...]
    late_ref[:, half + hid :] = wt_ref[...].T
    rank = uq_ref.shape[0]
    small_ref[:rank] = uq_ref[...]
    small_ref[rank : 2 * rank] = uv_ref[...]
    small_ref[2 * rank : 2 * rank + 1] = qb_ref[...].astype(F32).reshape(1, half)
    small_ref[2 * rank + 1 : 2 * rank + 2] = vb_ref[...].astype(F32).reshape(1, half)
    inner = ib_ref[...].astype(F32).reshape(1, hid)
    for k in range(hid // half):
        small_ref[2 * rank + 2 + k : 2 * rank + 3 + k] = inner[:, k * half : (k + 1) * half]
    for k, ref in enumerate((b0, b1, b2, b3, b4, b5)):
        vec_ref[k : k + 1] = ref[...].astype(F32).reshape(1, -1)
    count = bucket.shape[0]
    for m in range(count):
        place_of = 0
        for other in range(count):
            place_of += jnp.where(bucket[other] > bucket[m], 1, 0)
        outside = jnp.where((place_of == 0) | (place_of == count - 1), 0, 1)
        second = jnp.where(place_of >= count // 2, 1, 0)
        info_ref[(outside ^ here[1]) * 2 + second] = m
        info_ref[count + m] = bucket[m]
    info_ref[2 * count] = here[0]
    info_ref[2 * count + 1] = here[1]


def prepare(bucket, here, *arrays):
    wo, wi, wt, uq = arrays[:4]
    rows, half = wo.shape[1], wo.shape[0]
    smem = pl.BlockSpec(memory_space=pltpu.SMEM)
    vmem = pl.BlockSpec(memory_space=pltpu.VMEM)
    return pl.pallas_call(
        prepare_kernel,
        out_shape=(
            jax.ShapeDtypeStruct((rows, half + 2 * wi.shape[1]), BF16),
            jax.ShapeDtypeStruct((2 * uq.shape[0] + 2 + wi.shape[1] // half, half), F32),
            jax.ShapeDtypeStruct((8, arrays[8].shape[0]), F32),
            jax.ShapeDtypeStruct((2 * bucket.shape[0] + 2,), jnp.int32),
        ),
        in_specs=[smem, smem] + [vmem] * len(arrays),
        out_specs=(vmem, vmem, vmem, smem),
        cost_estimate=work(2e9),
        name="prepare",
    )(bucket, here, *arrays)


def split(a):
    high = a.astype(BF16)
    return high, (a - high.astype(F32)).astype(BF16)


def fwd_kernel(pos, count, info, x_ref, own_ref, peer_ref, qd_ref, vd_ref, live_ref, *rest):
    pieces, (qkv_ref, p_ref, ctx_ref, z_ref, w, wide_x, bias, sems) = rest[:count], rest[count:]
    slots, model, width = x_ref.shape[1], x_ref.shape[2], own_ref.shape[1]
    rank = qd_ref.shape[0]
    span, turn, pair = info[4 + info[pos]], pl.program_id(0), pl.program_id(1)
    half = info[9] ^ turn
    ((copies, early, late),) = fetch(pieces, info, [(0, 3 * width, stacked(w))], sems)

    @pl.when((turn == 0) & (pair == 0))
    def _():
        start_all(copies)
        t = lax.broadcasted_iota(jnp.int32, (slots, slots), 0)
        s = lax.broadcasted_iota(jnp.int32, (slots, slots), 1)
        ok = ((t ^ s) < span) & (live_ref[pl.ds(info[pos], 1), :] == 1)
        bias[...] = jnp.where(ok, 0.0, MASKED)
        down = jnp.concatenate([qd_ref[...], vd_ref[...]], axis=0)
        z = mm(x_ref[0], down, NT).astype(BF16)
        z_ref[0] = z
        wide_x[:, :model] = x_ref[0]
        wide_x[:, model:] = jnp.concatenate([z[:, :rank], z[:, :rank], z[:, rank:], z[:, rank:]], axis=1)
        wait_all(early)

    @pl.when((turn == 1) & (pair == 0))
    def _():
        wait_all(late)

    @pl.when(pair == 0)
    def _():
        rows, bq, bv = adapter_rows(own_ref, peer_ref, turn, rank)
        w[half, model:] = rows
        for k, shift in enumerate((bq, 0.0, bv)):
            cols = slice(k * width, (k + 1) * width)
            qkv_ref[0, :, cols] = (mm(wide_x[...], w[half, :, cols]) + shift).astype(BF16)

    masks = lane_masks()
    col = pl.multiple_of(pair * 128, 128)

    def attend(size):
        for b in range(slots // size):
            rows = slice(b * size, (b + 1) * size)
            q2 = qkv_ref[0, rows, pl.ds(col, 128)]
            k2 = qkv_ref[0, rows, pl.ds(width + col, 128)] * jnp.asarray(0.125, BF16)
            v2 = qkv_ref[0, rows, pl.ds(2 * width + col, 128)]
            acc = None
            for e in range(2):
                s = mm(q2, k2 * masks[e], NT) + bias[rows, rows]
                s = jnp.exp(s - jnp.max(s, axis=1, keepdims=True))
                probs = (s * (1.0 / jnp.sum(s, axis=1, keepdims=True))).astype(BF16)
                p_ref[0, e, rows, :size] = probs
                part = mm(probs, v2 * masks[e])
                acc = part if acc is None else acc + part
            ctx_ref[0, rows] = acc.astype(BF16)

    attend(block_size(pos, slots))


def block_size(pos, slots):
    return slots if pos == 0 else slots // 2


def any_spec():
    return pl.BlockSpec(memory_space=pl.ANY)


def sub_count(pieces):
    return sum(p.shape[0] for p in pieces)


def run_fwd(pos, info, tokens, pieces, small, peer_small, query_down, value_down, live):
    micro, slots, model = tokens.shape
    half = small.shape[1]
    pairs, wide = half // 128, slots if pos == 0 else slots // 2
    whole = lambda i, j, info: (0, 0)
    return pl.pallas_call(
        functools.partial(fwd_kernel, pos, len(pieces)),
        out_shape=(
            jax.ShapeDtypeStruct((2, slots, 3 * half), BF16),
            jax.ShapeDtypeStruct((2, 2 * pairs, slots, wide), BF16),
            jax.ShapeDtypeStruct((1, slots, model), BF16),
            jax.ShapeDtypeStruct((1, slots, 2 * query_down.shape[0]), BF16),
        ),
        grid_spec=pltpu.PrefetchScalarGridSpec(
            num_scalar_prefetch=1,
            grid=(2, pairs),
            in_specs=[
                pl.BlockSpec((1, slots, model), lambda i, j, info: (info[pos], 0, 0)),
                pl.BlockSpec(small.shape, whole),
                pl.BlockSpec(small.shape, whole),
                pl.BlockSpec(query_down.shape, whole),
                pl.BlockSpec(value_down.shape, whole),
                pl.BlockSpec(live.shape, whole),
            ]
            + [any_spec() for _ in pieces],
            out_specs=[
                pl.BlockSpec((1, slots, 3 * half), lambda i, j, info: (i ^ info[9], 0, 0)),
                pl.BlockSpec((1, 2, slots, wide), lambda i, j, info: (i ^ info[9], j, 0, 0)),
                pl.BlockSpec((1, slots, 128), lambda i, j, info: (0, 0, (i ^ info[9]) * pairs + j)),
                pl.BlockSpec((1, slots, 2 * query_down.shape[0]), lambda i, j, info: (0, 0, 0)),
            ],
            scratch_shapes=[
                pltpu.VMEM((2, model + 4 * query_down.shape[0], 3 * half), BF16),
                pltpu.VMEM((slots, model + 4 * query_down.shape[0]), BF16),
                pltpu.VMEM((slots, slots), F32),
                pltpu.SemaphoreType.DMA((sub_count(pieces),)),
            ],
        ),
        compiler_params=pltpu.CompilerParams(vmem_limit_bytes=VMEM),
        cost_estimate=work(12e9),
        name="attention_forward",
    )(info, tokens, small, peer_small, query_down, value_down, live, *pieces)


def gelu_parts(u):
    cdf = 0.5 * (1.0 + lax.erf(u * RSQRT2))
    pdf = jnp.exp(-0.5 * u * u) * PHI0
    return u * cdf, cdf + u * pdf


def norm(rows):
    c = rows - jnp.mean(rows, axis=1, keepdims=True)
    rstd = lax.rsqrt(jnp.mean(c * c, axis=1, keepdims=True) + EPS)
    return c * rstd, rstd


def norm_back(e, xhat, rstd):
    return rstd * (
        e - jnp.mean(e, axis=1, keepdims=True) - xhat * jnp.mean(e * xhat, axis=1, keepdims=True)
    )


def mid_kernel(pos, count, info, x_ref, ctx_ref, cot_ref, live_ref, own_ref, peer_ref, vec_ref, *rest):
    pieces = rest[:count]
    full_ref, act_ref, g1_ref, gctx_ref, wo, wi, wt, slope, xhat, acc, low, hidden, bi_ref, sems = rest[-14:]
    model = x_ref.shape[2]
    half, units = model // 2, wi.shape[1]
    hid, step = units // 2, 512
    parts = [
        (0, half, side_by_side(wo, half)),
        (half, hid, side_by_side(wi, hid)),
        (half + hid, hid, side_by_side(wt, hid)),
    ]
    fetched = fetch(pieces, info, parts, sems)
    for copies, _, _ in fetched:
        start_all(copies)
    first = own_ref.shape[0] - hid // half
    for h in range(2):
        small = jnp.where(info[9] == h, own_ref[...], peer_ref[...])
        for k in range(hid // half):
            cols = h * hid + k * half
            bi_ref[:, cols : cols + half] = small[first + k : first + k + 1]
    bo, b2 = vec_ref[0:1], vec_ref[1:2]
    s1, t1, s2, t2 = vec_ref[2:3], vec_ref[3:4], vec_ref[4:5], vec_ref[5:6]
    wait_all(fetched[0][1] + fetched[0][2])
    xh, rstd1 = norm(x_ref[0].astype(F32) + bo + mm(ctx_ref[0], wo[...], NT))
    xhat[...] = xh
    low[...] = (xh * s1 + t1).astype(BF16)
    wait_all(fetched[1][1] + fetched[1][2])

    def up(j, _):
        cols = pl.ds(pl.multiple_of(j * step, step), step)
        a, d = gelu_parts(mm(low[...], wi[:, cols]) + bi_ref[:, cols])
        slope[:, cols] = d
        hidden[:, cols] = a.astype(BF16)
        return 0

    lax.fori_loop(0, units // step, up, 0)
    wait_all(fetched[2][1] + fetched[2][2])
    xh2, rstd2 = norm(mm(hidden[...], wt[...], NT) + (xhat[...] * s1 + t1) + b2)
    act_ref[0] = (xh2 * s2 + t2).astype(BF16)
    full_ref[0] = act_ref[0]
    live = jnp.broadcast_to(live_ref[pl.ds(info[pos], 1), :].astype(F32), (8, live_ref.shape[1])).T[:, :1]
    g2 = norm_back(cot_ref[0].astype(F32) * live * s2, xh2, rstd2)
    low[...] = g2.astype(BF16)
    acc[...] = g2

    def down(j, _):
        cols = pl.ds(pl.multiple_of(j * step, step), step)
        hidden[:, cols] = (mm(low[...], wt[:, cols]) * slope[:, cols]).astype(BF16)
        return 0

    lax.fori_loop(0, units // step, down, 0)
    g1 = norm_back((acc[...] + mm(hidden[...], wi[...], NT)) * s1, xhat[...], rstd1)
    g1_ref[0] = g1
    gctx_ref[0] = mm(g1.astype(BF16), wo[...]).astype(BF16)


def run_mid(pos, info, tokens, ctx, cot, live, pieces, small, peer_small, vec, full):
    micro, slots, model = tokens.shape
    units = pieces[0].shape[-1] - model // 2
    own = lambda i, info: (info[pos], 0, 0)
    same = lambda i, info: (0, 0)
    in_specs = [
        pl.BlockSpec((1, slots, model), own),
        pl.BlockSpec((1, slots, model), lambda i, info: (0, 0, 0)),
        pl.BlockSpec((1, slots, model), own),
        pl.BlockSpec(live.shape, same, pipeline_mode=ONCE),
        pl.BlockSpec(small.shape, same, pipeline_mode=ONCE),
        pl.BlockSpec(small.shape, same, pipeline_mode=ONCE),
        pl.BlockSpec((8, model), same, pipeline_mode=ONCE),
    ] + [any_spec() for _ in pieces]
    args = [info, tokens, ctx, cot, live, small, peer_small, vec, *pieces]
    aliases = {}
    if full is not None:
        in_specs.append(any_spec())
        args.append(full)
        aliases = {len(args) - 1: 0}
    first = pl.BlockSpec((1, slots, model), lambda i, info: (0, 0, 0))
    return pl.pallas_call(
        functools.partial(mid_kernel, pos, len(pieces)),
        out_shape=(
            jax.ShapeDtypeStruct(tokens.shape, BF16),
            jax.ShapeDtypeStruct((1, slots, model), BF16),
            jax.ShapeDtypeStruct((1, slots, model), F32),
            jax.ShapeDtypeStruct((1, slots, model), BF16),
        ),
        grid_spec=pltpu.PrefetchScalarGridSpec(
            num_scalar_prefetch=1,
            grid=(1,),
            in_specs=in_specs,
            out_specs=[pl.BlockSpec((1, slots, model), own), first, first, first],
            scratch_shapes=[
                pltpu.VMEM((model, model), BF16),
                pltpu.VMEM((model, units), BF16),
                pltpu.VMEM((model, units), BF16),
                pltpu.VMEM((slots, units), F32),
                pltpu.VMEM((slots, model), F32),
                pltpu.VMEM((slots, model), F32),
                pltpu.VMEM((slots, model), BF16),
                pltpu.VMEM((slots, units), BF16),
                pltpu.VMEM((1, units), F32),
                pltpu.SemaphoreType.DMA((3 * sub_count(pieces),)),
            ],
        ),
        input_output_aliases=aliases,
        compiler_params=pltpu.CompilerParams(vmem_limit_bytes=VMEM),
        cost_estimate=work(24e9),
        name="feed_forward",
    )(*args)


def bwd_kernel(
    pos, count, info, qkv_ref, p_ref, z_ref, gctx_ref, g1_ref, own_ref, peer_ref, qd_ref, vd_ref, *rest
):
    pieces = rest[:count]
    full_ref, grad_ref, lora_ref, w, dqkv, total, sems = rest[-7:]
    slots, width = qkv_ref.shape[1], own_ref.shape[1]
    turn, pair = pl.program_id(0), pl.program_id(1)
    half = info[9] ^ turn
    masks = lane_masks()
    ((copies, early, late),) = fetch(pieces, info, [(0, 3 * width, stacked(w))], sems)

    @pl.when((turn == 0) & (pair == 0))
    def _():
        start_all(copies)

    col = pl.multiple_of(pair * 128, 128)

    def attend(size):
        for b in range(slots // size):
            rows = slice(b * size, (b + 1) * size)
            q2 = qkv_ref[0, rows, pl.ds(col, 128)] * jnp.asarray(0.125, BF16)
            k2 = qkv_ref[0, rows, pl.ds(width + col, 128)] * jnp.asarray(0.125, BF16)
            v2 = qkv_ref[0, rows, pl.ds(2 * width + col, 128)]
            g2 = gctx_ref[0, rows]
            dq = dk = dv = jnp.zeros((size, 128), F32)
            for e in range(2):
                probs = p_ref[0, e, rows, :size]
                dp = mm(g2, v2 * masks[e], NT)
                dv = dv + mm(probs, g2 * masks[e], TN)
                p32 = probs.astype(F32)
                pd = p32 * dp
                ds = (pd - p32 * jnp.sum(pd, axis=1, keepdims=True)).astype(BF16)
                dq = dq + mm(ds, k2 * masks[e])
                dk = dk + mm(ds, q2 * masks[e], TN)
            dqkv[rows, pl.ds(col, 128)] = dq.astype(BF16)
            dqkv[rows, pl.ds(width + col, 128)] = dk.astype(BF16)
            dqkv[rows, pl.ds(2 * width + col, 128)] = dv.astype(BF16)

    attend(block_size(pos, slots))

    @pl.when((turn == 0) & (pair == width // 128 - 1))
    def _():
        wait_all(early)

    @pl.when((turn == 1) & (pair == width // 128 - 1))
    def _():
        wait_all(late)

    @pl.when(pair == width // 128 - 1)
    def _():
        rank, model = qd_ref.shape[0], g1_ref.shape[2]
        w[half, model:] = adapter_rows(own_ref, peer_ref, turn, rank)[0]
        part = mm(dqkv[...], w[half], NT)
        t = part[:, model:]
        tq, tv = split(t[:, :rank] + t[:, rank : 2 * rank]), split(t[:, 2 * rank : 3 * rank] + t[:, 3 * rank :])
        down = jnp.concatenate([qd_ref[...], vd_ref[...]] * 2, axis=0)
        part = part[:, :model] + mm(jnp.concatenate([tq[0], tv[0], tq[1], tv[1]], axis=1), down)
        lora = 2.0 * mm(z_ref[0], dqkv[...], TN)
        lora_ref[0, :, :width] = lora[:rank, :width]
        lora_ref[0, :, width:] = lora[rank:, 2 * width :]

        @pl.when(turn == 0)
        def _():
            total[...] = g1_ref[0] + part

        @pl.when(turn == 1)
        def _():
            grad_ref[0] = (total[...] + part).astype(BF16)
            full_ref[0] = grad_ref[0]


def run_bwd(pos, info, qkv, probs, ctx, z, gctx, g1, pieces, small, peer_small, query_down, value_down, full):
    _, slots, width3 = qkv.shape
    half, model = width3 // 3, g1.shape[2]
    pairs, wide = half // 128, probs.shape[3]
    whole = lambda i, j, info: (0, 0)
    in_specs = [
        pl.BlockSpec((1, slots, width3), lambda i, j, info: (i ^ info[9], 0, 0)),
        pl.BlockSpec((1, 2, slots, wide), lambda i, j, info: (i ^ info[9], j, 0, 0)),
        pl.BlockSpec(z.shape, lambda i, j, info: (0, 0, 0)),
        pl.BlockSpec((1, slots, 128), lambda i, j, info: (0, 0, (i ^ info[9]) * pairs + j)),
        pl.BlockSpec((1, slots, model), lambda i, j, info: (0, 0, 0)),
        pl.BlockSpec(small.shape, whole),
        pl.BlockSpec(small.shape, whole),
        pl.BlockSpec(query_down.shape, whole),
        pl.BlockSpec(value_down.shape, whole),
    ] + [any_spec() for _ in pieces]
    args = [info, qkv, probs, z, gctx, g1, small, peer_small, query_down, value_down, *pieces]
    aliases = {}
    if full is not None:
        in_specs.append(any_spec())
        args.append(full)
        aliases = {len(args) - 1: 0}
    return pl.pallas_call(
        functools.partial(bwd_kernel, pos, len(pieces)),
        out_shape=(
            jax.ShapeDtypeStruct((4, slots, model), BF16),
            jax.ShapeDtypeStruct((1, slots, model), BF16),
            jax.ShapeDtypeStruct((2, query_down.shape[0], 2 * half), F32),
        ),
        grid_spec=pltpu.PrefetchScalarGridSpec(
            num_scalar_prefetch=1,
            grid=(2, pairs),
            in_specs=in_specs,
            out_specs=[
                pl.BlockSpec((1, slots, model), lambda i, j, info: (info[pos], 0, 0)),
                pl.BlockSpec((1, slots, model), lambda i, j, info: (0, 0, 0)),
                pl.BlockSpec((1, query_down.shape[0], 2 * half), lambda i, j, info: (i ^ info[9], 0, 0)),
            ],
            scratch_shapes=[
                pltpu.VMEM((2, model + 4 * query_down.shape[0], width3), BF16),
                pltpu.VMEM((slots, width3), BF16),
                pltpu.VMEM((slots, model), F32),
                pltpu.SemaphoreType.DMA((sub_count(pieces),)),
            ],
        ),
        input_output_aliases=aliases,
        compiler_params=pltpu.CompilerParams(vmem_limit_bytes=VMEM),
        cost_estimate=work(16e9),
        name="attention_backward",
    )(*args)


def place_kernel(pos, info, full_ref, *rest):
    pieces, (out_ref, sems) = rest[:-2], rest[-2:]
    copies = [
        pltpu.make_async_copy(piece.at[0], out_ref.at[info[2 + pos + n]], sems.at[n])
        for n, piece in enumerate(pieces)
    ]
    for copy in copies:
        copy.start()
    for copy in copies:
        copy.wait()


def place(pos, info, full, pieces):
    return pl.pallas_call(
        functools.partial(place_kernel, pos),
        out_shape=jax.ShapeDtypeStruct(full.shape, full.dtype),
        grid_spec=pltpu.PrefetchScalarGridSpec(
            num_scalar_prefetch=1,
            grid=(),
            in_specs=[any_spec()] + [pl.BlockSpec(memory_space=pltpu.VMEM) for _ in pieces],
            out_specs=any_spec(),
            scratch_shapes=[pltpu.SemaphoreType.DMA((len(pieces),))],
        ),
        input_output_aliases={1: 0},
        compiler_params=pltpu.CompilerParams(vmem_limit_bytes=8 << 20),
        cost_estimate=work(1e9),
        name="place",
    )(info, full, *pieces)


def sum_over_dp(a):
    size = lax.axis_size("dp")
    if size & (size - 1):
        return lax.psum(a, "dp")
    bit = 1
    while bit < size:
        a = a + lax.ppermute(a, "dp", [(i, i ^ bit) for i in range(size)])
        bit *= 2
    return a


def shards(
    tokens, live, bucket, query_weight, key_weight, value_weight, output_weight, inner_weight,
    outer_weight, query_bias, value_bias, output_bias, inner_bias, outer_bias, first_scale,
    first_bias, second_scale, second_bias, query_down, value_down, query_up, value_up, cotangent,
):
    micro, slots, model = tokens.shape
    half, hid = query_weight.shape[1], inner_weight.shape[1]
    rank = query_up.shape[0]
    me = lax.axis_index("head")
    size = lax.axis_size("dp")
    query_down, value_down = query_down.T, value_down.T
    here = jnp.stack([lax.axis_index("dp"), me]).astype(jnp.int32)
    early = pack([query_weight, key_weight, value_weight])
    late, small, vec, info = prepare(
        bucket, here, output_weight, inner_weight, outer_weight, query_up, value_up, query_bias, value_bias,
        inner_bias, output_bias, outer_bias, first_scale, first_bias, second_scale, second_bias,
    )
    peer_small = lax.ppermute(small, "head", SWAP)

    if by_permutes(size):
        go = permuter(size)

        def plane(pair, hold=None):
            across = go(pair, "first")
            return [pair, across, go(pair, "second"), go(across if hold is None else then(across, hold), "second")]

        def both_cores(blocks):
            return blocks + [go(block, "core") for block in blocks]

        ring = spread_ring(early, size)
        wqkv = []
        for k in (0, 2):
            wqkv += both_cores(plane(jnp.stack(ring[k : k + 2])))
        ring = spread_ring(then(late, ring[1]), size)
        near = plane(jnp.stack(ring[:2]))
        distant = jnp.stack(ring[2:])
    else:
        wqkv = gather_whole(early)
    first = run_fwd(0, info, tokens, wqkv, small, peer_small, query_down, value_down, live)
    if by_permutes(size):
        distant = plane(distant, first[2])
        wrest = both_cores(then(near, first[2]))
    else:
        wrest = gather_whole(late)
    second = run_fwd(1, then(info, first[2]), tokens, wqkv, small, peer_small, query_down, value_down, live)
    if by_permutes(size):
        wrest += both_cores(then(distant[:3], first[2]) + [then(distant[3], second[2])])
    acts = grads = None
    shared = (wqkv, small, peer_small, query_down, value_down)
    ctx = then(first[2], second[2])
    acts, a0, g1, gctx = run_mid(0, info, tokens, ctx, cotangent, live, wrest, small, peer_small, vec, acts)
    p_a0 = lax.ppermute(a0, "head", SWAP)
    grads, g0, lora0 = run_bwd(0, info, *first, gctx, g1, *shared, grads)
    p_g0 = lax.ppermute(g0, "head", SWAP)
    ctx = then(second[2], (p_a0, g0))
    acts, a1, g1, gctx = run_mid(1, info, tokens, ctx, cotangent, live, wrest, small, peer_small, vec, acts)
    p_a1 = lax.ppermute(a1, "head", SWAP)
    grads, g1, lora1 = run_bwd(1, info, *second, then(gctx, p_g0), g1, *shared, grads)
    p_g1 = lax.ppermute(then(g1, p_a1), "head", SWAP)
    lora = sum_over_dp(lora0 + lora1)
    mine, other = jnp.where(me == 0, lora, lora[::-1])
    acts = place(0, info, acts, [p_a0, p_a1])
    grads = place(0, info, grads, [p_g0])
    p_g1, other = then(p_g1, (acts, grads, lora)), then(other, p_g1)
    lora = mine + lax.ppermute(other, "head", SWAP)
    grads = place(1, info, grads, [p_g1])
    return acts, grads, lora[:, :half], lora[:, half:]


def solution(mesh):
    return jax.shard_map(
        shards,
        mesh=mesh,
        in_specs=(
            P(None, "dp", None), P(None, "dp"), P(),
            P("dp", "head"), P("dp", "head"), P("dp", "head"), P("head", "dp"), P("dp", "head"), P("head", "dp"),
            P("head"), P("head"), P(), P("head"), P(), P(), P(), P(), P(),
            P(), P(), P(None, "head"), P(None, "head"), P(None, "dp", None),
        ),
        out_specs=(P(None, "dp", None), P(None, "dp", None), P(None, "head"), P(None, "head")),
        check_vma=False,
    )
```

profile of v0, /device:TPU:0, one launch (start us, length us, event | category | flops | bytes accessed | tf_op | source)
XLA Modules:
  0.0 212.6 jit_solution(7869094411798736559)
XLA Ops:
  2.1 3.0 %collective-permute-start.1 = (bf16[48,1152]{1,0:T(8,128)(2,1)}, bf16[48,1152]{1,0:T(8,128)(2,1)S(1)}, u32[]{:S(2)}, u32[]{:S(2)}) collective-permute-start(bf16[48,1152]{1,0:T(8,128)(2,1)} %pack.1), channel_id=1, source_target_pairs={{0,8},{1,9},{2,10},{3,11},{4,12},{5,13},{6,14},{7,15},{8,16},{9,17... | collective-permute-start | bytes 331784 | tf_op jit(solution)/shard_map/ppermute | solution.py:54
  6.6 1.8 copy.33.wt_ref
  10.7 2.1 prepare.1
  12.8 1.6 collective-permute-start.18
  17.3 1.6 collective-permute-start.3
  18.9 7.5 %collective-permute-done.10 = bf16[48,1152]{1,0:T(8,128)(2,1)S(1)} collective-permute-done((bf16[48,1152]{1,0:T(8,128)(2,1)S(1)}, bf16[48,1152]{1,0:T(8,128)(2,1)S(1)}, u32[]{:S(2)}, u32[]{:S(2)}) %collective-permute-start.10) | collective-permute-done | bytes 110624 | tf_op jit(solution)/shard_map/ppermute | solution.py:54
  28.1 1.6 collective-permute-start.12
  30.2 3.3 %collective-permute-done.2.rest_1_ = bf16[2,48,1152]{2,1,0:T(8,128)(2,1)S(1)} collective-permute-done((bf16[2,48,1152]{2,1,0:T(8,128)(2,1)S(1)}, bf16[2,48,1152]{2,1,0:T(8,128)(2,1)S(1)}, u32[]{:S(2)}, u32[]{:S(2)}) %collective-permute-start.2) | collective-permute-done | bytes 221216 | tf_op jit(solution)/shard_map/ppermute | solution.py:54
  33.6 1.6 collective-permute-start.4
  41.8 2.7 %collective-permute-done.13.rest_11_ = bf16[2,48,1152]{2,1,0:T(8,128)(2,1)S(1)} collective-permute-done((bf16[2,48,1152]{2,1,0:T(8,128)(2,1)S(1)}, bf16[2,48,1152]{2,1,0:T(8,128)(2,1)S(1)}, u32[]{:S(2)}, u32[]{:S(2)}) %collective-permute-start.13) | collective-permute-done | bytes 221216 | tf_op jit(solution)/shard_map/ppermute | solution.py:54
  44.5 4.9 %collective-permute-done.27 = bf16[48,3456]{1,0:T(8,128)(2,1)S(1)} collective-permute-done((bf16[48,3456]{1,0:T(8,128)(2,1)S(1)}, bf16[48,3456]{1,0:T(8,128)(2,1)S(1)}, u32[]{:S(2)}, u32[]{:S(2)}) %collective-permute-start.27) | collective-permute-done | bytes 331808 | tf_op jit(solution)/shard_map/ppermute | solution.py:54
  53.3 19.1 %attention_forward.2 = (bf16[2,512,1152]{2,1,0:T(8,128)(2,1)}, bf16[2,6,512,512]{3,2,1,0:T(8,128)(2,1)}, bf16[1,512,768]{2,1,0:T(8,128)(2,1)}, bf16[1,512,16]{2,1,0:T(8,128)(2,1)}) custom-call(s32[10]{0:T(128)} %get-tuple-element.50.info, bf16[4,512,768]{2,1,0:T(8,128)(2,1)} %x_ref.7, f32[22,384]{1,0:T(8,128)} %get-tuple-element.48.own_ref, ...), custom_call_target="tpu_custom_call" | custom-call | flops 12000000000 | bytes 8388608 | tf_op jit(solution)/shard_map/attention_forward/pallas_call | solution.py:298
  72.5 1.6 collective-permute-start.29
  76.5 15.5 %attention_forward.3 = (bf16[2,512,1152]{2,1,0:T(8,128)(2,1)}, bf16[2,6,512,256]{3,2,1,0:T(8,128)(2,1)}, bf16[1,512,768]{2,1,0:T(8,128)(2,1)}, bf16[1,512,16]{2,1,0:T(8,128)(2,1)}) custom-call(s32[10]{0:T(128)} %get-tuple-element.50.info, bf16[4,512,768]{2,1,0:T(8,128)(2,1)} %x_ref.7, f32[22,384]{1,0:T(8,128)} %get-tuple-element.48.own_ref, ...), custom_call_target="tpu_custom_call" | custom-call | flops 12000000000 | bytes 8388608 | tf_op jit(solution)/shard_map/attention_forward/pallas_call | solution.py:298
  94.5 1.7 collective-permute-done.31.rest_12_
  99.1 24.4 %feed_forward.2 = (bf16[4,512,768]{2,1,0:T(8,128)(2,1)}, bf16[1,512,768]{2,1,0:T(8,128)(2,1)}, f32[1,512,768]{2,1,0:T(8,128)}, bf16[1,512,768]{2,1,0:T(8,128)(2,1)}) custom-call(s32[10]{0:T(128)} %get-tuple-element.50.info, bf16[4,512,768]{2,1,0:T(8,128)(2,1)} %x_ref.7, bf16[1,512,768]{2,1,0:T(8,128)(2,1)} %get-tuple-element.52.ctx_ref, ...), custom_call_target="tpu_custom_call" | custom-call | flops 24000000000 | bytes 8388608 | tf_op jit(solution)/shard_map/feed_forward/pallas_call | solution.py:432
  124.2 19.8 %attention_backward.2 = (bf16[4,512,768]{2,1,0:T(8,128)(2,1)}, bf16[1,512,768]{2,1,0:T(8,128)(2,1)}, f32[2,8,768]{2,1,0:T(8,128)}) custom-call(s32[10]{0:T(128)} %get-tuple-element.50.info, bf16[2,512,1152]{2,1,0:T(8,128)(2,1)} %get-tuple-element.66.qkv_ref, bf16[2,6,512,512]{3,2,1,0:T(8,128)(2,1)} %get-tuple-element.67.p_ref, ...), custom_call_target="tpu_custom_call" | custom-call | flops 16000000000 | bytes 8388608 | tf_op jit(solution)/shard_map/attention_backward/pallas_call | solution.py:558
  145.4 24.4 %feed_forward.3 = (bf16[4,512,768]{2,1,0:T(8,128)(2,1)}, bf16[1,512,768]{2,1,0:T(8,128)(2,1)}, f32[1,512,768]{2,1,0:T(8,128)}, bf16[1,512,768]{2,1,0:T(8,128)(2,1)}) custom-call(s32[10]{0:T(128)} %get-tuple-element.50.info, bf16[4,512,768]{2,1,0:T(8,128)(2,1)} %x_ref.7, ...), custom_call_target="tpu_custom_call", output_to_operand_aliasing={{0}: (24, {})} | custom-call | flops 24000000000 | bytes 8388608 | tf_op jit(solution)/shard_map/feed_forward/pallas_call | solution.py:432
  170.6 16.5 %attention_backward.3 = (bf16[4,512,768]{2,1,0:T(8,128)(2,1)}, bf16[1,512,768]{2,1,0:T(8,128)(2,1)}, f32[2,8,768]{2,1,0:T(8,128)}) custom-call(s32[10]{0:T(128)} %get-tuple-element.50.info, bf16[2,512,1152]{2,1,0:T(8,128)(2,1)} %get-tuple-element.76.qkv_ref, bf16[2,6,512,256]{3,2,1,0:T(8,128)(2,1)} %get-tuple-element.77.p_ref, ...), custom_call_target="tpu_custom_call", output_to_operand_aliasing={{0}: (26, {})} | custom-call | flops 16000000000 | bytes 8388608 | tf_op jit(solution)/shard_map/attention_backward/pallas_call | solution.py:558
  191.2 3.0 %collective-permute-done.40 = f32[2,8,768]{2,1,0:T(8,128)S(1)} collective-permute-done((f32[2,8,768]{2,1,0:T(8,128)S(1)}, f32[2,8,768]{2,1,0:T(8,128)S(1)}, u32[]{:S(2)}, u32[]{:S(2)}) %collective-permute-start.40) | collective-permute-done | bytes 49184 | tf_op jit(solution)/shard_map/ppermute | solution.py:624
  194.2 2.0 collective-permute-start.41
  196.2 2.2 %collective-permute-done.41 = f32[2,8,768]{2,1,0:T(8,128)S(1)} collective-permute-done((f32[2,8,768]{2,1,0:T(8,128)S(1)}, f32[2,8,768]{2,1,0:T(8,128)S(1)}, u32[]{:S(2)}, u32[]{:S(2)}) %collective-permute-start.41) | collective-permute-done | bytes 49184 | tf_op jit(solution)/shard_map/ppermute | solution.py:624
  198.4 4.7 %collective-permute-start.42 = (f32[2,8,768]{2,1,0:T(8,128)S(1)}, f32[2,8,768]{2,1,0:T(8,128)S(1)}, u32[]{:S(2)}, u32[]{:S(2)}) collective-permute-start(f32[2,8,768]{2,1,0:T(8,128)S(1)} %add.21), channel_id=1, source_target_pairs={{0,16},{2,18},{4,20},{6,22},{8,24},{10,26},{12,28},{14,30},{16,0},... | collective-permute-start | bytes 147464 | tf_op jit(solution)/shard_map/ppermute | solution.py:624
  205.3 1.7 place.3
  (149 shorter events, 43.2 us)
Async XLA Ops:
  2.1 8.3 %collective-permute-start.1 = (bf16[48,1152]{1,0:T(8,128)(2,1)}, bf16[48,1152]{1,0:T(8,128)(2,1)S(1)}, u32[]{:S(2)}, u32[]{:S(2)}) collective-permute-start(bf16[48,1152]{1,0:T(8,128)(2,1)} %pack.1), channel_id=1, source_target_pairs={{0,8},{1,9},{2,10},{3,11},{4,12},{5,13},{6,14},{7,15},{8,16},{9,17... | collective-permute-start | bytes 331784 | tf_op jit(solution)/shard_map/ppermute | solution.py:54
  12.8 15.1 %collective-permute-start.18 = (bf16[48,3456]{1,0:T(8,128)(2,1)}, bf16[48,3456]{1,0:T(8,128)(2,1)S(1)}, u32[]{:S(2)}, u32[]{:S(2)}) collective-permute-start(bf16[48,3456]{1,0:T(8,128)(2,1)} %get-tuple-element.55), channel_id=1, source_target_pairs={{0,8},{1,9},{2,10},{3,11},{4,12},{5,13},{6,14},{7,15},{8,16},{9,17... | collective-permute-start | bytes 995336 | tf_op jit(solution)/shard_map/ppermute | solution.py:54
  14.4 13.5 %collective-permute-start = (f32[22,384]{1,0:T(8,128)}, f32[22,384]{1,0:T(8,128)S(1)}, u32[]{:S(2)}, u32[]{:S(2)}) collective-permute-start(f32[22,384]{1,0:T(8,128)} %get-tuple-element.48.own_ref), channel_id=1, source_target_pairs={{0,1},{1,0},{2,3},{3,2},{4,5},{5,4},{6,7},{7,6},{8,9},{9,8},{10,11... | collective-permute-start | bytes 101384 | tf_op jit(solution)/shard_map/ppermute | solution.py:646
  17.2 9.3 %collective-permute-start.10 = (bf16[48,1152]{1,0:T(8,128)(2,1)S(1)}, bf16[48,1152]{1,0:T(8,128)(2,1)S(1)}, u32[]{:S(2)}, u32[]{:S(2)}) collective-permute-start(bf16[48,1152]{1,0:T(8,128)(2,1)S(1)} %collective-permute-done.9), channel_id=1, source_target_pairs={{0,8},{1,9},{2,10},{3,11},{4,12},{5,13},{6,14},{7,15},{8,16},{9,17... | collective-permute-start | bytes 331784 | tf_op jit(solution)/shard_map/ppermute | solution.py:54
  17.2 10.8 %collective-permute-start.5 = (bf16[2,48,1152]{2,1,0:T(8,128)(2,1)S(1)}, bf16[2,48,1152]{2,1,0:T(8,128)(2,1)S(1)}, u32[]{:S(2)}, u32[]{:S(2)}) collective-permute-start(bf16[2,48,1152]{2,1,0:T(8,128)(2,1)S(1)} %pad_maximum_fusion.2.rest_0_), channel_id=1, source_target_pairs={{0,2},{1,3},{2,0},{3,1},{4,6},{5,7},{6,4},{7,5},{8,10},{9,11},{10,... | collective-permute-start | bytes 663560 | tf_op jit(solution)/shard_map/ppermute | solution.py:54
  17.3 12.4 %collective-permute-start.3 = (bf16[2,48,1152]{2,1,0:T(8,128)(2,1)S(1)}, bf16[2,48,1152]{2,1,0:T(8,128)(2,1)S(1)}, u32[]{:S(2)}, u32[]{:S(2)}) collective-permute-start(bf16[2,48,1152]{2,1,0:T(8,128)(2,1)S(1)} %pad_maximum_fusion.2.rest_0_), channel_id=1, source_target_pairs={{0,1},{1,0},{2,6},{3,7},{4,5},{5,4},{6,2},{7,3},{8,9},{9,8},{10,14... | collective-permute-start | bytes 663560 | tf_op jit(solution)/shard_map/ppermute | solution.py:54
  27.9 10.7 %collective-permute-start.26 = (bf16[48,3456]{1,0:T(8,128)(2,1)S(1)}, bf16[48,3456]{1,0:T(8,128)(2,1)S(1)}, u32[]{:S(2)}, u32[]{:S(2)}) collective-permute-start(bf16[48,3456]{1,0:T(8,128)(2,1)S(1)} %collective-permute-done.18), channel_id=1, source_target_pairs={{0,8},{1,9},{2,10},{3,11},{4,12},{5,13},{6,14},{7,15},{8,16},{9,17... | collective-permute-start | bytes 995336 | tf_op jit(solution)/shard_map/ppermute | solution.py:54
  28.1 8.1 %collective-permute-start.12 = (bf16[2,48,1152]{2,1,0:T(8,128)(2,1)S(1)}, bf16[2,48,1152]{2,1,0:T(8,128)(2,1)S(1)}, u32[]{:S(2)}, u32[]{:S(2)}) collective-permute-start(bf16[2,48,1152]{2,1,0:T(8,128)(2,1)S(1)} %pad_maximum_fusion.3.rest_8_), channel_id=1, source_target_pairs={{0,1},{1,0},{2,6},{3,7},{4,5},{5,4},{6,2},{7,3},{8,9},{9,8},{10,14... | collective-permute-start | bytes 663560 | tf_op jit(solution)/shard_map/ppermute | solution.py:54
  38.6 10.7 %collective-permute-start.27 = (bf16[48,3456]{1,0:T(8,128)(2,1)S(1)}, bf16[48,3456]{1,0:T(8,128)(2,1)S(1)}, u32[]{:S(2)}, u32[]{:S(2)}) collective-permute-start(bf16[48,3456]{1,0:T(8,128)(2,1)S(1)} %collective-permute-done.26), channel_id=1, source_target_pairs={{0,8},{1,9},{2,10},{3,11},{4,12},{5,13},{6,14},{7,15},{8,16},{9,17... | collective-permute-start | bytes 995336 | tf_op jit(solution)/shard_map/ppermute | solution.py:54
  39.7 12.2 %collective-permute-start.19 = (bf16[2,48,3456]{2,1,0:T(8,128)(2,1)S(1)}, bf16[2,48,3456]{2,1,0:T(8,128)(2,1)S(1)}, u32[]{:S(2)}, u32[]{:S(2)}) collective-permute-start(bf16[2,48,3456]{2,1,0:T(8,128)(2,1)S(1)} %pad_maximum_fusion.rest_0_), channel_id=1, source_target_pairs={{0,4},{1,5},{2,3},{3,2},{4,0},{5,1},{6,7},{7,6},{8,12},{9,13},{10,... | collective-permute-start | bytes 1990664 | tf_op jit(solution)/shard_map/ppermute | solution.py:54
  41.3 9.7 %collective-permute-start.15 = (bf16[2,48,1152]{2,1,0:T(8,128)(2,1)S(1)}, bf16[2,48,1152]{2,1,0:T(8,128)(2,1)S(1)}, u32[]{:S(2)}, u32[]{:S(2)}) collective-permute-start(bf16[2,48,1152]{2,1,0:T(8,128)(2,1)S(1)} %collective-permute-done.11.rest_9_), channel_id=1, source_target_pairs={{0,2},{1,3},{2,0},{3,1},{4,6},{5,7},{6,4},{7,5},{8,10},{9,11},{10,... | collective-permute-start | bytes 663560 | tf_op jit(solution)/shard_map/ppermute | solution.py:54
  41.3 8.2 %collective-permute-start.16 = (bf16[2,48,1152]{2,1,0:T(8,128)(2,1)S(1)}, bf16[2,48,1152]{2,1,0:T(8,128)(2,1)S(1)}, u32[]{:S(2)}, u32[]{:S(2)}) collective-permute-start(bf16[2,48,1152]{2,1,0:T(8,128)(2,1)S(1)} %collective-permute-done.12.rest_10_), channel_id=1, source_target_pairs={{0,2},{1,3},{2,0},{3,1},{4,6},{5,7},{6,4},{7,5},{8,10},{9,11},{10,... | collective-permute-start | bytes 663560 | tf_op jit(solution)/shard_map/ppermute | solution.py:54
  49.5 24.6 %collective-permute-start.20 = (bf16[2,48,3456]{2,1,0:T(8,128)(2,1)S(1)}, bf16[2,48,3456]{2,1,0:T(8,128)(2,1)S(1)}, u32[]{:S(2)}, u32[]{:S(2)}) collective-permute-start(bf16[2,48,3456]{2,1,0:T(8,128)(2,1)S(1)} %pad_maximum_fusion.rest_0_), channel_id=1, source_target_pairs={{0,1},{1,0},{2,6},{3,7},{4,5},{5,4},{6,2},{7,3},{8,9},{9,8},{10,14... | collective-permute-start | bytes 1990664 | tf_op jit(solution)/shard_map/ppermute | solution.py:54
  51.0 23.1 %collective-permute-start.28 = (bf16[2,48,3456]{2,1,0:T(8,128)(2,1)S(1)}, bf16[2,48,3456]{2,1,0:T(8,128)(2,1)}, u32[]{:S(2)}, u32[]{:S(2)}) collective-permute-start(bf16[2,48,3456]{2,1,0:T(8,128)(2,1)S(1)} %pad_maximum_fusion.1.rest_8_), channel_id=1, source_target_pairs={{0,4},{1,5},{2,3},{3,2},{4,0},{5,1},{6,7},{7,6},{8,12},{9,13},{10,... | collective-permute-start | bytes 1990664 | tf_op jit(solution)/shard_map/ppermute | solution.py:54
  52.0 22.6 %collective-permute-start.21 = (bf16[2,48,3456]{2,1,0:T(8,128)(2,1)S(1)}, bf16[2,48,3456]{2,1,0:T(8,128)(2,1)}, u32[]{:S(2)}, u32[]{:S(2)}) collective-permute-start(bf16[2,48,3456]{2,1,0:T(8,128)(2,1)S(1)} %collective-permute-done.19.rest_1_), channel_id=1, source_target_pairs={{0,1},{1,0},{2,6},{3,7},{4,5},{5,4},{6,2},{7,3},{8,9},{9,8},{10,14... | collective-permute-start | bytes 1990664 | tf_op jit(solution)/shard_map/ppermute | solution.py:54
  72.5 19.6 %collective-permute-start.29 = (bf16[2,48,3456]{2,1,0:T(8,128)(2,1)S(1)}, bf16[2,48,3456]{2,1,0:T(8,128)(2,1)}, u32[]{:S(2)}, u32[]{:S(2)}) collective-permute-start(bf16[2,48,3456]{2,1,0:T(8,128)(2,1)S(1)} %pad_maximum_fusion.1.rest_8_), channel_id=1, source_target_pairs={{0,1},{1,0},{2,6},{3,7},{4,5},{5,4},{6,2},{7,3},{8,9},{9,8},{10,14... | collective-permute-start | bytes 1990664 | tf_op jit(solution)/shard_map/ppermute | solution.py:54
  74.6 18.1 %collective-permute-start.22 = (bf16[2,48,3456]{2,1,0:T(8,128)(2,1)S(1)}, bf16[2,48,3456]{2,1,0:T(8,128)(2,1)}, u32[]{:S(2)}, u32[]{:S(2)}) collective-permute-start(bf16[2,48,3456]{2,1,0:T(8,128)(2,1)S(1)} %pad_maximum_fusion.rest_0_), channel_id=1, source_target_pairs={{0,2},{1,3},{2,0},{3,1},{4,6},{5,7},{6,4},{7,5},{8,10},{9,11},{10,... | collective-permute-start | bytes 1990664 | tf_op jit(solution)/shard_map/ppermute | solution.py:54
  74.6 18.2 %collective-permute-start.23 = (bf16[2,48,3456]{2,1,0:T(8,128)(2,1)S(1)}, bf16[2,48,3456]{2,1,0:T(8,128)(2,1)}, u32[]{:S(2)}, u32[]{:S(2)}) collective-permute-start(bf16[2,48,3456]{2,1,0:T(8,128)(2,1)S(1)} %collective-permute-done.19.rest_1_), channel_id=1, source_target_pairs={{0,2},{1,3},{2,0},{3,1},{4,6},{5,7},{6,4},{7,5},{8,10},{9,11},{10,... | collective-permute-start | bytes 1990664 | tf_op jit(solution)/shard_map/ppermute | solution.py:54
  75.1 18.1 %collective-permute-start.24 = (bf16[2,48,3456]{2,1,0:T(8,128)(2,1)S(1)}, bf16[2,48,3456]{2,1,0:T(8,128)(2,1)}, u32[]{:S(2)}, u32[]{:S(2)}) collective-permute-start(bf16[2,48,3456]{2,1,0:T(8,128)(2,1)S(1)} %collective-permute-done.20.rest_2_), channel_id=1, source_target_pairs={{0,2},{1,3},{2,0},{3,1},{4,6},{5,7},{6,4},{7,5},{8,10},{9,11},{10,... | collective-permute-start | bytes 1990664 | tf_op jit(solution)/shard_map/ppermute | solution.py:54
  75.2 17.0 %collective-permute-start.30 = (bf16[2,48,3456]{2,1,0:T(8,128)(2,1)}, bf16[2,48,3456]{2,1,0:T(8,128)(2,1)}, u32[]{:S(2)}, u32[]{:S(2)}) collective-permute-start(bf16[2,48,3456]{2,1,0:T(8,128)(2,1)} %collective-permute-done.28.rest_9_), channel_id=1, source_target_pairs={{0,1},{1,0},{2,6},{3,7},{4,5},{5,4},{6,2},{7,3},{8,9},{9,8},{10,14... | collective-permute-start | bytes 1990664 | tf_op jit(solution)/shard_map/ppermute | solution.py:54
  123.4 22.0 %collective-permute-start.35 = (bf16[1,512,768]{2,1,0:T(8,128)(2,1)}, bf16[1,512,768]{2,1,0:T(8,128)(2,1)S(1)}, u32[]{:S(2)}, u32[]{:S(2)}) collective-permute-start(bf16[1,512,768]{2,1,0:T(8,128)(2,1)} %get-tuple-element.65), channel_id=1, source_target_pairs={{0,1},{1,0},{2,3},{3,2},{4,5},{5,4},{6,7},{7,6},{8,9},{9,8},{10,11... | collective-permute-start | bytes 2359304 | tf_op jit(solution)/shard_map/ppermute | solution.py:680
  144.1 25.8 %collective-permute-start.37 = (bf16[1,512,768]{2,1,0:T(8,128)(2,1)}, bf16[1,512,768]{2,1,0:T(8,128)(2,1)S(1)}, u32[]{:S(2)}, u32[]{:S(2)}) collective-permute-start(bf16[1,512,768]{2,1,0:T(8,128)(2,1)} %get-tuple-element.71), channel_id=1, source_target_pairs={{0,1},{1,0},{2,3},{3,2},{4,5},{5,4},{6,7},{7,6},{8,9},{9,8},{10,11... | collective-permute-start | bytes 2359304 | tf_op jit(solution)/shard_map/ppermute | solution.py:682
  169.8 19.3 %collective-permute-start.36 = (bf16[1,512,768]{2,1,0:T(8,128)(2,1)}, bf16[1,512,768]{2,1,0:T(8,128)(2,1)S(1)}, u32[]{:S(2)}, u32[]{:S(2)}) collective-permute-start(bf16[1,512,768]{2,1,0:T(8,128)(2,1)} %get-tuple-element.75), channel_id=1, source_target_pairs={{0,1},{1,0},{2,3},{3,2},{4,5},{5,4},{6,7},{7,6},{8,9},{9,8},{10,11... | collective-permute-start | bytes 2359304 | tf_op jit(solution)/shard_map/ppermute | solution.py:685
  189.1 19.1 %collective-permute-start.38 = (bf16[1,512,768]{2,1,0:T(8,128)(2,1)}, bf16[1,512,768]{2,1,0:T(8,128)(2,1)S(1)}, u32[]{:S(2)}, u32[]{:S(2)}) collective-permute-start(bf16[1,512,768]{2,1,0:T(8,128)(2,1)} %get-tuple-element.85), channel_id=1, source_target_pairs={{0,1},{1,0},{2,3},{3,2},{4,5},{5,4},{6,7},{7,6},{8,9},{9,8},{10,11... | collective-permute-start | bytes 2359304 | tf_op jit(solution)/shard_map/ppermute | solution.py:687
  (49 other events, 518.1 us)
where the time goes:
time: 214 us; the launch traced here: 213 us
  Pallas kernels  128 us (60%)
  starting transfers between devices  37.7 us (18%)
  waiting for transfers between devices  37.1 us (17%)
  local copies, waits for them, and re-layouts  6.22 us (3%)
  other arithmetic  2.67 us (1%)
    pallas_call x2, Pallas kernels, run_mid(): pl.pallas_call(functools.partial(mid_kernel, pos, len(pieces)), out_shape...  48.7 us
    pallas_call x2, Pallas kernels, run_bwd(): pl.pallas_call(functools.partial(bwd_kernel, pos, len(pieces)), out_shape...  36.3 us
    pallas_call x2, Pallas kernels, run_fwd(): pl.pallas_call(functools.partial(fwd_kernel, pos, len(pieces)), out_shape...  34.6 us
    ppermute x34, waiting for transfers between devices, permuter(): return lambda a, which: lax.ppermute(a, ('dp', 'head'), tables[which])  27.7 us
    ppermute x34, starting transfers between devices, permuter(): return lambda a, which: lax.ppermute(a, ('dp', 'head'), tables[which])  23.2 us
    ppermute x4, starting transfers between devices, sum_over_dp(): a = a + lax.ppermute(a, 'dp', [(i, i ^ bit) for i in range(size)])  7.77 us
    ppermute x4, waiting for transfers between devices, sum_over_dp(): a = a + lax.ppermute(a, 'dp', [(i, i ^ bit) for i in range(size)])  6.03 us
    unnamed x60, local copies, waits for them, and re-layouts  5.6 us
  transfers between devices with their start and end apart: 44, of which 20 were waited for; matrix products, arithmetic and copies ran while one was open for 3% of the time, Pallas kernels for 48%

commit v1 on v0

--- a/solution.py
+++ b/solution.py
@@ -73,7 +73,7 @@
 def sub_pieces(refs, info):
     dp, y = info[8], info[9]
     if len(refs) == 1:
-        return [(refs[0].at[y ^ h], y ^ h, 0, h) for h in range(2)]
+        return [(refs[0].at[y ^ h], h, 0) for h in range(2)]
     rows = refs[0].shape[1]
     z, x, core = dp >> 2, (dp >> 1) & 1, dp & 1
     out = []
@@ -84,42 +84,19 @@
             for j in range(4):
                 dx, dy = ((0, 0), (1 - c, c), (c, 1 - c), (1, 1))[j]
                 row = (deep + ((x ^ dx) << 1) + c) * rows
-                view = refs[(k // 2) * 8 + side * 4 + j].at[k % 2]
-                slot = dy * 16 + (k * 2 + side) * 2 + (1 if j in (1, 2) else 0)
-                out.append((view, y ^ dy, pl.multiple_of(row, rows), slot))
+                out.append((refs[(k // 2) * 8 + side * 4 + j].at[k % 2], dy, pl.multiple_of(row, rows)))
     return out
 
 
 def fetch(refs, info, parts, sems):
-    subs = sub_pieces(refs, info)
-    count = len(subs)
-    result = []
     for p, (start, cols, dest) in enumerate(parts):
-        copies = [
-            pltpu.make_async_copy(
-                ref.at[:, pl.ds(start, cols)], dest(h, row, ref.shape[0]), sems.at[p * count + slot]
-            )
-            for ref, h, row, slot in subs
-        ]
-        ref, h, row, _ = subs[0]
-        waits = [
-            pltpu.make_async_copy(
-                ref.at[:, pl.ds(start, cols)], dest(h, row, ref.shape[0]), sems.at[p * count + slot]
-            )
-            for slot in range(count)
-        ]
-        result.append((copies, waits[: count // 2], waits[count // 2 :]))
-    return result
-
-
-def start_all(copies):
-    for copy in copies:
-        copy.start()
-
-
-def wait_all(copies):
-    for copy in copies:
-        copy.wait()
+        for ref, dy, row in sub_pieces(refs, info):
+            view = ref.at[:, pl.ds(start, cols)]
+            pltpu.make_async_copy(view, dest(info[9] ^ dy, row, ref.shape[0]), sems.at[2 * p + dy]).start()
+
+
+def wait_for(buf, sem):
+    pltpu.make_async_copy(buf, buf, sem).wait()
 
 
 def side_by_side(buf, count):
@@ -170,10 +147,10 @@
     bucket, here, wo_ref, wi_ref, wt_ref, uq_ref, uv_ref, qb_ref, vb_ref, ib_ref,
     b0, b1, b2, b3, b4, b5, late_ref, small_ref, vec_ref, info_ref,
 ):
-    half, hid = wo_ref.shape[0], wi_ref.shape[1]
-    late_ref[:, :half] = wo_ref[...].T
+    half, hid = wo_ref.shape[1], wi_ref.shape[1]
+    late_ref[:, :half] = wo_ref[...]
     late_ref[:, half : half + hid] = wi_ref[...]
-    late_ref[:, half + hid :] = wt_ref[...].T
+    late_ref[:, half + hid :] = wt_ref[...]
     rank = uq_ref.shape[0]
     small_ref[:rank] = uq_ref[...]
     small_ref[rank : 2 * rank] = uv_ref[...]
@@ -199,7 +176,7 @@
 
 def prepare(bucket, here, *arrays):
     wo, wi, wt, uq = arrays[:4]
-    rows, half = wo.shape[1], wo.shape[0]
+    rows, half = wo.shape
     smem = pl.BlockSpec(memory_space=pltpu.SMEM)
     vmem = pl.BlockSpec(memory_space=pltpu.VMEM)
     return pl.pallas_call(
@@ -228,11 +205,10 @@
     rank = qd_ref.shape[0]
     span, turn, pair = info[4 + info[pos]], pl.program_id(0), pl.program_id(1)
     half = info[9] ^ turn
-    ((copies, early, late),) = fetch(pieces, info, [(0, 3 * width, stacked(w))], sems)
 
     @pl.when((turn == 0) & (pair == 0))
     def _():
-        start_all(copies)
+        fetch(pieces, info, [(0, 3 * width, stacked(w))], sems)
         t = lax.broadcasted_iota(jnp.int32, (slots, slots), 0)
         s = lax.broadcasted_iota(jnp.int32, (slots, slots), 1)
         ok = ((t ^ s) < span) & (live_ref[pl.ds(info[pos], 1), :] == 1)
@@ -242,14 +218,10 @@
         z_ref[0] = z
         wide_x[:, :model] = x_ref[0]
         wide_x[:, model:] = jnp.concatenate([z[:, :rank], z[:, :rank], z[:, rank:], z[:, rank:]], axis=1)
-        wait_all(early)
-
-    @pl.when((turn == 1) & (pair == 0))
-    def _():
-        wait_all(late)
 
     @pl.when(pair == 0)
     def _():
+        wait_for(w.at[half, :model], sems.at[turn])
         rows, bq, bv = adapter_rows(own_ref, peer_ref, turn, rank)
         w[half, model:] = rows
         for k, shift in enumerate((bq, 0.0, bv)):
@@ -284,10 +256,6 @@
 
 def any_spec():
     return pl.BlockSpec(memory_space=pl.ANY)
-
-
-def sub_count(pieces):
-    return sum(p.shape[0] for p in pieces)
 
 
 def run_fwd(pos, info, tokens, pieces, small, peer_small, query_down, value_down, live):
@@ -325,7 +293,7 @@
                 pltpu.VMEM((2, model + 4 * query_down.shape[0], 3 * half), BF16),
                 pltpu.VMEM((slots, model + 4 * query_down.shape[0]), BF16),
                 pltpu.VMEM((slots, slots), F32),
-                pltpu.SemaphoreType.DMA((sub_count(pieces),)),
+                pltpu.SemaphoreType.DMA((2,)),
             ],
         ),
         compiler_params=pltpu.CompilerParams(vmem_limit_bytes=VMEM),
@@ -357,15 +325,13 @@
     full_ref, act_ref, g1_ref, gctx_ref, wo, wi, wt, slope, xhat, acc, low, hidden, bi_ref, sems = rest[-14:]
     model = x_ref.shape[2]
     half, units = model // 2, wi.shape[1]
-    hid, step = units // 2, 512
+    hid, step = units // 2, 768
     parts = [
         (0, half, side_by_side(wo, half)),
         (half, hid, side_by_side(wi, hid)),
         (half + hid, hid, side_by_side(wt, hid)),
     ]
-    fetched = fetch(pieces, info, parts, sems)
-    for copies, _, _ in fetched:
-        start_all(copies)
+    fetch(pieces, info, parts, sems)
     first = own_ref.shape[0] - hid // half
     for h in range(2):
         small = jnp.where(info[9] == h, own_ref[...], peer_ref[...])
@@ -374,11 +340,13 @@
             bi_ref[:, cols : cols + half] = small[first + k : first + k + 1]
     bo, b2 = vec_ref[0:1], vec_ref[1:2]
     s1, t1, s2, t2 = vec_ref[2:3], vec_ref[3:4], vec_ref[4:5], vec_ref[5:6]
-    wait_all(fetched[0][1] + fetched[0][2])
+    for h in range(2):
+        wait_for(wo.at[:, h * half : (h + 1) * half], sems.at[0 + h])
     xh, rstd1 = norm(x_ref[0].astype(F32) + bo + mm(ctx_ref[0], wo[...], NT))
     xhat[...] = xh
     low[...] = (xh * s1 + t1).astype(BF16)
-    wait_all(fetched[1][1] + fetched[1][2])
+    for h in range(2):
+        wait_for(wi.at[:, h * hid : (h + 1) * hid], sems.at[2 + h])
 
     def up(j, _):
         cols = pl.ds(pl.multiple_of(j * step, step), step)
@@ -388,7 +356,8 @@
         return 0
 
     lax.fori_loop(0, units // step, up, 0)
-    wait_all(fetched[2][1] + fetched[2][2])
+    for h in range(2):
+        wait_for(wt.at[:, h * hid : (h + 1) * hid], sems.at[4 + h])
     xh2, rstd2 = norm(mm(hidden[...], wt[...], NT) + (xhat[...] * s1 + t1) + b2)
     act_ref[0] = (xh2 * s2 + t2).astype(BF16)
     full_ref[0] = act_ref[0]
@@ -452,7 +421,7 @@
                 pltpu.VMEM((slots, model), BF16),
                 pltpu.VMEM((slots, units), BF16),
                 pltpu.VMEM((1, units), F32),
-                pltpu.SemaphoreType.DMA((3 * sub_count(pieces),)),
+                pltpu.SemaphoreType.DMA((6,)),
             ],
         ),
         input_output_aliases=aliases,
@@ -471,11 +440,10 @@
     turn, pair = pl.program_id(0), pl.program_id(1)
     half = info[9] ^ turn
     masks = lane_masks()
-    ((copies, early, late),) = fetch(pieces, info, [(0, 3 * width, stacked(w))], sems)
 
     @pl.when((turn == 0) & (pair == 0))
     def _():
-        start_all(copies)
+        fetch(pieces, info, [(0, 3 * width, stacked(w))], sems)
 
     col = pl.multiple_of(pair * 128, 128)
 
@@ -502,34 +470,29 @@
 
     attend(block_size(pos, slots))
 
-    @pl.when((turn == 0) & (pair == width // 128 - 1))
-    def _():
-        wait_all(early)
-
-    @pl.when((turn == 1) & (pair == width // 128 - 1))
-    def _():
-        wait_all(late)
-
     @pl.when(pair == width // 128 - 1)
     def _():
         rank, model = qd_ref.shape[0], g1_ref.shape[2]
+        wait_for(w.at[half, :model], sems.at[turn])
         w[half, model:] = adapter_rows(own_ref, peer_ref, turn, rank)[0]
         part = mm(dqkv[...], w[half], NT)
-        t = part[:, model:]
-        tq, tv = split(t[:, :rank] + t[:, rank : 2 * rank]), split(t[:, 2 * rank : 3 * rank] + t[:, 3 * rank :])
-        down = jnp.concatenate([qd_ref[...], vd_ref[...]] * 2, axis=0)
-        part = part[:, :model] + mm(jnp.concatenate([tq[0], tv[0], tq[1], tv[1]], axis=1), down)
         lora = 2.0 * mm(z_ref[0], dqkv[...], TN)
         lora_ref[0, :, :width] = lora[:rank, :width]
         lora_ref[0, :, width:] = lora[rank:, 2 * width :]
 
         @pl.when(turn == 0)
         def _():
-            total[...] = g1_ref[0] + part
+            total[:, :model] = g1_ref[0] + part[:, :model]
+            total[:, model:] = part[:, model:]
 
         @pl.when(turn == 1)
         def _():
-            grad_ref[0] = (total[...] + part).astype(BF16)
+            t = total[:, model:] + part[:, model:]
+            tq, tv = split(t[:, :rank] + t[:, rank : 2 * rank]), split(t[:, 2 * rank : 3 * rank] + t[:, 3 * rank :])
+            down = jnp.concatenate([qd_ref[...], vd_ref[...]] * 2, axis=0)
+            sums = total[:, :model] + part[:, :model]
+            sums = sums + mm(jnp.concatenate([tq[0], tv[0], tq[1], tv[1]], axis=1), down)
+            grad_ref[0] = sums.astype(BF16)
             full_ref[0] = grad_ref[0]
 
 
@@ -574,8 +537,8 @@
             scratch_shapes=[
                 pltpu.VMEM((2, model + 4 * query_down.shape[0], width3), BF16),
                 pltpu.VMEM((slots, width3), BF16),
-                pltpu.VMEM((slots, model), F32),
-                pltpu.SemaphoreType.DMA((sub_count(pieces),)),
+                pltpu.VMEM((slots, model + 4 * query_down.shape[0]), F32),
+                pltpu.SemaphoreType.DMA((2,)),
             ],
         ),
         input_output_aliases=aliases,
@@ -640,7 +603,7 @@
     here = jnp.stack([lax.axis_index("dp"), me]).astype(jnp.int32)
     early = pack([query_weight, key_weight, value_weight])
     late, small, vec, info = prepare(
-        bucket, here, output_weight, inner_weight, outer_weight, query_up, value_up, query_bias, value_bias,
+        bucket, here, output_weight.T, inner_weight, outer_weight.T, query_up, value_up, query_bias, value_bias,
         inner_bias, output_bias, outer_bias, first_scale, first_bias, second_scale, second_bias,
     )
     peer_small = lax.ppermute(small, "head", SWAP)
@@ -648,9 +611,10 @@
     if by_permutes(size):
         go = permuter(size)
 
-        def plane(pair, hold=None):
-            across = go(pair, "first")
-            return [pair, across, go(pair, "second"), go(across if hold is None else then(across, hold), "second")]
+        def plane(pair, flip, hold=None):
+            one, two = go(pair, "first"), go(pair, "second")
+            via, last = (two, "first") if flip else (one, "second")
+            return [pair, one, two, go(via if hold is None else then(via, hold), last)]
 
         def both_cores(blocks):
             return blocks + [go(block, "core") for block in blocks]
@@ -658,15 +622,15 @@
         ring = spread_ring(early, size)
         wqkv = []
         for k in (0, 2):
-            wqkv += both_cores(plane(jnp.stack(ring[k : k + 2])))
+            wqkv += both_cores(plane(jnp.stack(ring[k : k + 2]), k == 2))
         ring = spread_ring(then(late, ring[1]), size)
-        near = plane(jnp.stack(ring[:2]))
+        near = plane(jnp.stack(ring[:2]), False)
         distant = jnp.stack(ring[2:])
     else:
         wqkv = gather_whole(early)
     first = run_fwd(0, info, tokens, wqkv, small, peer_small, query_down, value_down, live)
     if by_permutes(size):
-        distant = plane(distant, first[2])
+        distant = plane(distant, True, first[2])
         wrest = both_cores(then(near, first[2]))
     else:
         wrest = gather_whole(late)
@@ -676,15 +640,17 @@
     acts = grads = None
     shared = (wqkv, small, peer_small, query_down, value_down)
     ctx = then(first[2], second[2])
-    acts, a0, g1, gctx = run_mid(0, info, tokens, ctx, cotangent, live, wrest, small, peer_small, vec, acts)
+    acts, a0, g1_0, gctx0 = run_mid(0, info, tokens, ctx, cotangent, live, wrest, small, peer_small, vec, acts)
     p_a0 = lax.ppermute(a0, "head", SWAP)
-    grads, g0, lora0 = run_bwd(0, info, *first, gctx, g1, *shared, grads)
+    ctx = then(second[2], a0)
+    acts, a1, g1_1, gctx1 = run_mid(1, info, tokens, ctx, cotangent, live, wrest, small, peer_small, vec, acts)
+    p_a1 = lax.ppermute(a1, "head", SWAP)
+    gctx0 = then(gctx0, (p_a0, a1))
+    grads, g0, lora0 = run_bwd(0, info, *first, gctx0, g1_0, *shared, grads)
     p_g0 = lax.ppermute(g0, "head", SWAP)
-    ctx = then(second[2], (p_a0, g0))
-    acts, a1, g1, gctx = run_mid(1, info, tokens, ctx, cotangent, live, wrest, small, peer_small, vec, acts)
-    p_a1 = lax.ppermute(a1, "head", SWAP)
-    grads, g1, lora1 = run_bwd(1, info, *second, then(gctx, p_g0), g1, *shared, grads)
-    p_g1 = lax.ppermute(then(g1, p_a1), "head", SWAP)
+    gctx1 = then(gctx1, (p_a1, g0))
+    grads, g1, lora1 = run_bwd(1, info, *second, gctx1, g1_1, *shared, grads)
+    p_g1 = lax.ppermute(then(g1, p_g0), "head", SWAP)
     lora = sum_over_dp(lora0 + lora1)
     mine, other = jnp.where(me == 0, lora, lora[::-1])
     acts = place(0, info, acts, [p_a0, p_a1])

time: 214 us -> 208 us (0.972)
  waiting for transfers between devices: 37.1 us -> 44.9 us
  Pallas kernels: 128 us -> 121 us
  local copies, waits for them, and re-layouts: 6.22 us -> 2.36 us
  starting transfers between devices: 37.7 us -> 34.5 us
    ppermute x34, waiting for transfers between devices: 27.7 us -> 33.8 us  [permuter(): return lambda a, which: lax.ppermute(a, ('dp', 'head'), tables[which])]
    unnamed x60 -> x58, local copies, waits for them, and re-layouts: 5.6 us -> 1.75 us
    pallas_call x2, Pallas kernels: 48.7 us -> 45.5 us  [run_mid(): pl.pallas_call(functools.partial(mid_kernel, pos, len(pieces)), out_shape...]
    pallas_call x2, Pallas kernels: 36.3 us -> 34.1 us  [run_bwd(): pl.pallas_call(functools.partial(bwd_kernel, pos, len(pieces)), out_shape...]
  transfers between devices with their start and end apart: 44 -> 44, of which waited for: 20 -> 20; matrix products, arithmetic and copies ran while one was open for 3% -> 1% of each run, Pallas kernels for 48% -> 47%
where the time goes in v1:
time: 208 us; the launch traced here: 207 us
  Pallas kernels  121 us (58%)
  waiting for transfers between devices  44.9 us (22%)
  starting transfers between devices  34.5 us (17%)
  other arithmetic  2.6 us (1%)
  local copies, waits for them, and re-layouts  2.36 us (1%)
    pallas_call x2, Pallas kernels, run_mid(): pl.pallas_call(functools.partial(mid_kernel, pos, len(pieces)), out_shape...  45.5 us
    pallas_call x2, Pallas kernels, run_bwd(): pl.pallas_call(functools.partial(bwd_kernel, pos, len(pieces)), out_shape...  34.1 us
    ppermute x34, waiting for transfers between devices, permuter(): return lambda a, which: lax.ppermute(a, ('dp', 'head'), tables[which])  33.8 us
    pallas_call x2, Pallas kernels, run_fwd(): pl.pallas_call(functools.partial(fwd_kernel, pos, len(pieces)), out_shape...  33.8 us
    ppermute x34, starting transfers between devices, permuter(): return lambda a, which: lax.ppermute(a, ('dp', 'head'), tables[which])  21.5 us
    ppermute x4, starting transfers between devices, sum_over_dp(): a = a + lax.ppermute(a, 'dp', [(i, i ^ bit) for i in range(size)])  6.44 us
    ppermute x4, waiting for transfers between devices, sum_over_dp(): a = a + lax.ppermute(a, 'dp', [(i, i ^ bit) for i in range(size)])  6.4 us
    pallas_call x3, Pallas kernels, place(): pl.pallas_call(functools.partial(place_kernel, pos), out_shape=jax.ShapeD...  4.56 us
  transfers between devices with their start and end apart: 44, of which 20 were waited for; matrix products, arithmetic and copies ran while one was open for 1% of the time, Pallas kernels for 47%

profile of v1, /device:TPU:0, one launch (start us, length us, event | category | flops | bytes accessed | tf_op | source)
XLA Modules:
  0.0 206.8 jit_solution(7086065410987534593)
XLA Ops:
  2.1 3.0 %collective-permute-start.1 = (bf16[48,1152]{1,0:T(8,128)(2,1)}, bf16[48,1152]{1,0:T(8,128)(2,1)S(1)}, u32[]{:S(2)}, u32[]{:S(2)}) collective-permute-start(bf16[48,1152]{1,0:T(8,128)(2,1)} %pack.1), channel_id=1, source_target_pairs={{0,8},{1,9},{2,10},{3,11},{4,12},{5,13},{6,14},{7,15},{8,16},{9,17... | collective-permute-start | bytes 331784 | tf_op jit(solution)/shard_map/ppermute | solution.py:54
  5.7 4.7 %collective-permute-done.1 = bf16[48,1152]{1,0:T(8,128)(2,1)S(1)} collective-permute-done((bf16[48,1152]{1,0:T(8,128)(2,1)}, bf16[48,1152]{1,0:T(8,128)(2,1)S(1)}, u32[]{:S(2)}, u32[]{:S(2)}) %collective-permute-start.1) | collective-permute-done | bytes 110624 | tf_op jit(solution)/shard_map/ppermute | solution.py:54
  10.4 1.9 prepare.1
  15.2 2.5 %collective-permute-done.9 = bf16[48,1152]{1,0:T(8,128)(2,1)S(1)} collective-permute-done((bf16[48,1152]{1,0:T(8,128)(2,1)S(1)}, bf16[48,1152]{1,0:T(8,128)(2,1)S(1)}, u32[]{:S(2)}, u32[]{:S(2)}) %collective-permute-start.9) | collective-permute-done | bytes 110624 | tf_op jit(solution)/shard_map/ppermute | solution.py:54
  17.9 1.8 collective-permute-start.3
  19.6 6.8 %collective-permute-done.10 = bf16[48,1152]{1,0:T(8,128)(2,1)S(1)} collective-permute-done((bf16[48,1152]{1,0:T(8,128)(2,1)S(1)}, bf16[48,1152]{1,0:T(8,128)(2,1)S(1)}, u32[]{:S(2)}, u32[]{:S(2)}) %collective-permute-start.10) | collective-permute-done | bytes 110624 | tf_op jit(solution)/shard_map/ppermute | solution.py:54
  28.1 1.6 collective-permute-start.12
  30.2 3.3 %collective-permute-done.2.rest_1_ = bf16[2,48,1152]{2,1,0:T(8,128)(2,1)S(1)} collective-permute-done((bf16[2,48,1152]{2,1,0:T(8,128)(2,1)S(1)}, bf16[2,48,1152]{2,1,0:T(8,128)(2,1)S(1)}, u32[]{:S(2)}, u32[]{:S(2)}) %collective-permute-start.2) | collective-permute-done | bytes 221216 | tf_op jit(solution)/shard_map/ppermute | solution.py:54
  33.6 1.6 collective-permute-start.4
  41.4 1.6 collective-permute-done.13.rest_11_
  43.0 6.7 %collective-permute-done.27 = bf16[48,3456]{1,0:T(8,128)(2,1)S(1)} collective-permute-done((bf16[48,3456]{1,0:T(8,128)(2,1)S(1)}, bf16[48,3456]{1,0:T(8,128)(2,1)S(1)}, u32[]{:S(2)}, u32[]{:S(2)}) %collective-permute-start.27) | collective-permute-done | bytes 331808 | tf_op jit(solution)/shard_map/ppermute | solution.py:54
  53.4 19.0 %attention_forward.2 = (bf16[2,512,1152]{2,1,0:T(8,128)(2,1)}, bf16[2,6,512,512]{3,2,1,0:T(8,128)(2,1)}, bf16[1,512,768]{2,1,0:T(8,128)(2,1)}, bf16[1,512,16]{2,1,0:T(8,128)(2,1)}) custom-call(s32[10]{0:T(128)} %get-tuple-element.51.info, bf16[4,512,768]{2,1,0:T(8,128)(2,1)} %x_ref.7, f32[22,384]{1,0:T(8,128)} %get-tuple-element.49.own_ref, ...), custom_call_target="tpu_custom_call" | custom-call | flops 12000000000 | bytes 8388608 | tf_op jit(solution)/shard_map/attention_forward/pallas_call | solution.py:266
  76.5 14.8 %attention_forward.3 = (bf16[2,512,1152]{2,1,0:T(8,128)(2,1)}, bf16[2,6,512,256]{3,2,1,0:T(8,128)(2,1)}, bf16[1,512,768]{2,1,0:T(8,128)(2,1)}, bf16[1,512,16]{2,1,0:T(8,128)(2,1)}) custom-call(s32[10]{0:T(128)} %get-tuple-element.51.info, bf16[4,512,768]{2,1,0:T(8,128)(2,1)} %x_ref.7, f32[22,384]{1,0:T(8,128)} %get-tuple-element.49.own_ref, ...), custom_call_target="tpu_custom_call" | custom-call | flops 12000000000 | bytes 8388608 | tf_op jit(solution)/shard_map/attention_forward/pallas_call | solution.py:266
  93.8 1.7 collective-permute-done.31.rest_12_
  95.7 1.7 collective-permute-done.33.rest_14_
  98.4 22.8 %feed_forward.2 = (bf16[4,512,768]{2,1,0:T(8,128)(2,1)}, bf16[1,512,768]{2,1,0:T(8,128)(2,1)}, f32[1,512,768]{2,1,0:T(8,128)}, bf16[1,512,768]{2,1,0:T(8,128)(2,1)}) custom-call(s32[10]{0:T(128)} %get-tuple-element.51.info, bf16[4,512,768]{2,1,0:T(8,128)(2,1)} %x_ref.7, bf16[1,512,768]{2,1,0:T(8,128)(2,1)} %get-tuple-element.53.ctx_ref, ...), custom_call_target="tpu_custom_call" | custom-call | flops 24000000000 | bytes 8388608 | tf_op jit(solution)/shard_map/feed_forward/pallas_call | solution.py:401
  122.0 22.8 %feed_forward.3 = (bf16[4,512,768]{2,1,0:T(8,128)(2,1)}, bf16[1,512,768]{2,1,0:T(8,128)(2,1)}, f32[1,512,768]{2,1,0:T(8,128)}, bf16[1,512,768]{2,1,0:T(8,128)(2,1)}) custom-call(s32[10]{0:T(128)} %get-tuple-element.51.info, bf16[4,512,768]{2,1,0:T(8,128)(2,1)} %x_ref.7, ...), custom_call_target="tpu_custom_call", output_to_operand_aliasing={{0}: (24, {})} | custom-call | flops 24000000000 | bytes 8388608 | tf_op jit(solution)/shard_map/feed_forward/pallas_call | solution.py:401
  146.2 18.6 %attention_backward.2 = (bf16[4,512,768]{2,1,0:T(8,128)(2,1)}, bf16[1,512,768]{2,1,0:T(8,128)(2,1)}, f32[2,8,768]{2,1,0:T(8,128)}) custom-call(s32[10]{0:T(128)} %get-tuple-element.51.info, bf16[2,512,1152]{2,1,0:T(8,128)(2,1)} %get-tuple-element.75.qkv_ref, bf16[2,6,512,512]{3,2,1,0:T(8,128)(2,1)} %get-tuple-element.76.p_ref, ...), custom_call_target="tpu_custom_call" | custom-call | flops 16000000000 | bytes 8388608 | tf_op jit(solution)/shard_map/attention_backward/pallas_call | solution.py:521
  165.6 15.5 %attention_backward.3 = (bf16[4,512,768]{2,1,0:T(8,128)(2,1)}, bf16[1,512,768]{2,1,0:T(8,128)(2,1)}, f32[2,8,768]{2,1,0:T(8,128)}) custom-call(s32[10]{0:T(128)} %get-tuple-element.51.info, bf16[2,512,1152]{2,1,0:T(8,128)(2,1)} %get-tuple-element.71.qkv_ref, bf16[2,6,512,256]{3,2,1,0:T(8,128)(2,1)} %get-tuple-element.72.p_ref, ...), custom_call_target="tpu_custom_call", output_to_operand_aliasing={{0}: (26, {})} | custom-call | flops 16000000000 | bytes 8388608 | tf_op jit(solution)/shard_map/attention_backward/pallas_call | solution.py:521
  181.9 2.1 %collective-permute-done.37.rest_0_ = bf16[1,512,768]{2,1,0:T(8,128)(2,1)S(1)} collective-permute-done((bf16[1,512,768]{2,1,0:T(8,128)(2,1)}, bf16[1,512,768]{2,1,0:T(8,128)(2,1)S(1)}, u32[]{:S(2)}, u32[]{:S(2)}) %collective-permute-start.37) | collective-permute-done | bytes 786464 | tf_op jit(solution)/shard_map/ppermute | solution.py:650
  186.1 3.1 %collective-permute-done.40 = f32[2,8,768]{2,1,0:T(8,128)S(1)} collective-permute-done((f32[2,8,768]{2,1,0:T(8,128)S(1)}, f32[2,8,768]{2,1,0:T(8,128)S(1)}, u32[]{:S(2)}, u32[]{:S(2)}) %collective-permute-start.40) | collective-permute-done | bytes 49184 | tf_op jit(solution)/shard_map/ppermute | solution.py:587
  190.3 3.0 %collective-permute-done.41 = f32[2,8,768]{2,1,0:T(8,128)S(1)} collective-permute-done((f32[2,8,768]{2,1,0:T(8,128)S(1)}, f32[2,8,768]{2,1,0:T(8,128)S(1)}, u32[]{:S(2)}, u32[]{:S(2)}) %collective-permute-start.41) | collective-permute-done | bytes 49184 | tf_op jit(solution)/shard_map/ppermute | solution.py:587
  193.3 4.2 %collective-permute-start.42 = (f32[2,8,768]{2,1,0:T(8,128)S(1)}, f32[2,8,768]{2,1,0:T(8,128)S(1)}, u32[]{:S(2)}, u32[]{:S(2)}) collective-permute-start(f32[2,8,768]{2,1,0:T(8,128)S(1)} %add.21), channel_id=1, source_target_pairs={{0,16},{2,18},{4,20},{6,22},{8,24},{10,26},{12,28},{14,30},{16,0},... | collective-permute-start | bytes 147464 | tf_op jit(solution)/shard_map/ppermute | solution.py:587
  197.5 1.7 place.3
  (147 shorter events, 39.3 us)
Async XLA Ops:
  2.1 8.3 %collective-permute-start.1 = (bf16[48,1152]{1,0:T(8,128)(2,1)}, bf16[48,1152]{1,0:T(8,128)(2,1)S(1)}, u32[]{:S(2)}, u32[]{:S(2)}) collective-permute-start(bf16[48,1152]{1,0:T(8,128)(2,1)} %pack.1), channel_id=1, source_target_pairs={{0,8},{1,9},{2,10},{3,11},{4,12},{5,13},{6,14},{7,15},{8,16},{9,17... | collective-permute-start | bytes 331784 | tf_op jit(solution)/shard_map/ppermute | solution.py:54
  12.3 15.6 %collective-permute-start.18 = (bf16[48,3456]{1,0:T(8,128)(2,1)}, bf16[48,3456]{1,0:T(8,128)(2,1)S(1)}, u32[]{:S(2)}, u32[]{:S(2)}) collective-permute-start(bf16[48,3456]{1,0:T(8,128)(2,1)} %get-tuple-element.56), channel_id=1, source_target_pairs={{0,8},{1,9},{2,10},{3,11},{4,12},{5,13},{6,14},{7,15},{8,16},{9,17... | collective-permute-start | bytes 995336 | tf_op jit(solution)/shard_map/ppermute | solution.py:54
  13.7 14.3 %collective-permute-start = (f32[22,384]{1,0:T(8,128)}, f32[22,384]{1,0:T(8,128)S(1)}, u32[]{:S(2)}, u32[]{:S(2)}) collective-permute-start(f32[22,384]{1,0:T(8,128)} %get-tuple-element.49.own_ref), channel_id=1, source_target_pairs={{0,1},{1,0},{2,3},{3,2},{4,5},{5,4},{6,7},{7,6},{8,9},{9,8},{10,11... | collective-permute-start | bytes 101384 | tf_op jit(solution)/shard_map/ppermute | solution.py:609
  17.7 8.7 %collective-permute-start.10 = (bf16[48,1152]{1,0:T(8,128)(2,1)S(1)}, bf16[48,1152]{1,0:T(8,128)(2,1)S(1)}, u32[]{:S(2)}, u32[]{:S(2)}) collective-permute-start(bf16[48,1152]{1,0:T(8,128)(2,1)S(1)} %collective-permute-done.9), channel_id=1, source_target_pairs={{0,8},{1,9},{2,10},{3,11},{4,12},{5,13},{6,14},{7,15},{8,16},{9,17... | collective-permute-start | bytes 331784 | tf_op jit(solution)/shard_map/ppermute | solution.py:54
  17.8 10.3 %collective-permute-start.5 = (bf16[2,48,1152]{2,1,0:T(8,128)(2,1)S(1)}, bf16[2,48,1152]{2,1,0:T(8,128)(2,1)S(1)}, u32[]{:S(2)}, u32[]{:S(2)}) collective-permute-start(bf16[2,48,1152]{2,1,0:T(8,128)(2,1)S(1)} %pad_maximum_fusion.2.rest_0_), channel_id=1, source_target_pairs={{0,2},{1,3},{2,0},{3,1},{4,6},{5,7},{6,4},{7,5},{8,10},{9,11},{10,... | collective-permute-start | bytes 663560 | tf_op jit(solution)/shard_map/ppermute | solution.py:54
  17.9 11.8 %collective-permute-start.3 = (bf16[2,48,1152]{2,1,0:T(8,128)(2,1)S(1)}, bf16[2,48,1152]{2,1,0:T(8,128)(2,1)S(1)}, u32[]{:S(2)}, u32[]{:S(2)}) collective-permute-start(bf16[2,48,1152]{2,1,0:T(8,128)(2,1)S(1)} %pad_maximum_fusion.2.rest_0_), channel_id=1, source_target_pairs={{0,1},{1,0},{2,6},{3,7},{4,5},{5,4},{6,2},{7,3},{8,9},{9,8},{10,14... | collective-permute-start | bytes 663560 | tf_op jit(solution)/shard_map/ppermute | solution.py:54
  27.9 10.7 %collective-permute-start.26 = (bf16[48,3456]{1,0:T(8,128)(2,1)S(1)}, bf16[48,3456]{1,0:T(8,128)(2,1)S(1)}, u32[]{:S(2)}, u32[]{:S(2)}) collective-permute-start(bf16[48,3456]{1,0:T(8,128)(2,1)S(1)} %collective-permute-done.18), channel_id=1, source_target_pairs={{0,8},{1,9},{2,10},{3,11},{4,12},{5,13},{6,14},{7,15},{8,16},{9,17... | collective-permute-start | bytes 995336 | tf_op jit(solution)/shard_map/ppermute | solution.py:54
  38.6 11.1 %collective-permute-start.27 = (bf16[48,3456]{1,0:T(8,128)(2,1)S(1)}, bf16[48,3456]{1,0:T(8,128)(2,1)S(1)}, u32[]{:S(2)}, u32[]{:S(2)}) collective-permute-start(bf16[48,3456]{1,0:T(8,128)(2,1)S(1)} %collective-permute-done.26), channel_id=1, source_target_pairs={{0,8},{1,9},{2,10},{3,11},{4,12},{5,13},{6,14},{7,15},{8,16},{9,17... | collective-permute-start | bytes 995336 | tf_op jit(solution)/shard_map/ppermute | solution.py:54
  39.7 12.3 %collective-permute-start.19 = (bf16[2,48,3456]{2,1,0:T(8,128)(2,1)S(1)}, bf16[2,48,3456]{2,1,0:T(8,128)(2,1)S(1)}, u32[]{:S(2)}, u32[]{:S(2)}) collective-permute-start(bf16[2,48,3456]{2,1,0:T(8,128)(2,1)S(1)} %pad_maximum_fusion.rest_0_), channel_id=1, source_target_pairs={{0,4},{1,5},{2,3},{3,2},{4,0},{5,1},{6,7},{7,6},{8,12},{9,13},{10,... | collective-permute-start | bytes 1990664 | tf_op jit(solution)/shard_map/ppermute | solution.py:54
  40.9 9.0 %collective-permute-start.16 = (bf16[2,48,1152]{2,1,0:T(8,128)(2,1)S(1)}, bf16[2,48,1152]{2,1,0:T(8,128)(2,1)}, u32[]{:S(2)}, u32[]{:S(2)}) collective-permute-start(bf16[2,48,1152]{2,1,0:T(8,128)(2,1)S(1)} %collective-permute-done.12.rest_10_), channel_id=1, source_target_pairs={{0,2},{1,3},{2,0},{3,1},{4,6},{5,7},{6,4},{7,5},{8,10},{9,11},{10,... | collective-permute-start | bytes 663560 | tf_op jit(solution)/shard_map/ppermute | solution.py:54
  40.9 9.5 %collective-permute-start.15 = (bf16[2,48,1152]{2,1,0:T(8,128)(2,1)S(1)}, bf16[2,48,1152]{2,1,0:T(8,128)(2,1)S(1)}, u32[]{:S(2)}, u32[]{:S(2)}) collective-permute-start(bf16[2,48,1152]{2,1,0:T(8,128)(2,1)S(1)} %collective-permute-done.11.rest_9_), channel_id=1, source_target_pairs={{0,2},{1,3},{2,0},{3,1},{4,6},{5,7},{6,4},{7,5},{8,10},{9,11},{10,... | collective-permute-start | bytes 663560 | tf_op jit(solution)/shard_map/ppermute | solution.py:54
  43.0 9.5 %collective-permute-start.8 = (bf16[2,48,1152]{2,1,0:T(8,128)(2,1)S(1)}, bf16[2,48,1152]{2,1,0:T(8,128)(2,1)S(1)}, u32[]{:S(2)}, u32[]{:S(2)}) collective-permute-start(bf16[2,48,1152]{2,1,0:T(8,128)(2,1)S(1)} %collective-permute-done.4.rest_3_), channel_id=1, source_target_pairs={{0,2},{1,3},{2,0},{3,1},{4,6},{5,7},{6,4},{7,5},{8,10},{9,11},{10,... | collective-permute-start | bytes 663560 | tf_op jit(solution)/shard_map/ppermute | solution.py:54
  49.9 23.8 %collective-permute-start.20 = (bf16[2,48,3456]{2,1,0:T(8,128)(2,1)S(1)}, bf16[2,48,3456]{2,1,0:T(8,128)(2,1)S(1)}, u32[]{:S(2)}, u32[]{:S(2)}) collective-permute-start(bf16[2,48,3456]{2,1,0:T(8,128)(2,1)S(1)} %pad_maximum_fusion.rest_0_), channel_id=1, source_target_pairs={{0,1},{1,0},{2,6},{3,7},{4,5},{5,4},{6,2},{7,3},{8,9},{9,8},{10,14... | collective-permute-start | bytes 1990664 | tf_op jit(solution)/shard_map/ppermute | solution.py:54
  50.4 23.2 %collective-permute-start.29 = (bf16[2,48,3456]{2,1,0:T(8,128)(2,1)S(1)}, bf16[2,48,3456]{2,1,0:T(8,128)(2,1)S(1)}, u32[]{:S(2)}, u32[]{:S(2)}) collective-permute-start(bf16[2,48,3456]{2,1,0:T(8,128)(2,1)S(1)} %pad_maximum_fusion.1.rest_8_), channel_id=1, source_target_pairs={{0,1},{1,0},{2,6},{3,7},{4,5},{5,4},{6,2},{7,3},{8,9},{9,8},{10,14... | collective-permute-start | bytes 1990664 | tf_op jit(solution)/shard_map/ppermute | solution.py:54
  52.0 22.9 %collective-permute-start.21 = (bf16[2,48,3456]{2,1,0:T(8,128)(2,1)S(1)}, bf16[2,48,3456]{2,1,0:T(8,128)(2,1)}, u32[]{:S(2)}, u32[]{:S(2)}) collective-permute-start(bf16[2,48,3456]{2,1,0:T(8,128)(2,1)S(1)} %collective-permute-done.19.rest_1_), channel_id=1, source_target_pairs={{0,1},{1,0},{2,6},{3,7},{4,5},{5,4},{6,2},{7,3},{8,9},{9,8},{10,14... | collective-permute-start | bytes 1990664 | tf_op jit(solution)/shard_map/ppermute | solution.py:54
  72.4 19.0 %collective-permute-start.28 = (bf16[2,48,3456]{2,1,0:T(8,128)(2,1)S(1)}, bf16[2,48,3456]{2,1,0:T(8,128)(2,1)}, u32[]{:S(2)}, u32[]{:S(2)}) collective-permute-start(bf16[2,48,3456]{2,1,0:T(8,128)(2,1)S(1)} %pad_maximum_fusion.1.rest_8_), channel_id=1, source_target_pairs={{0,4},{1,5},{2,3},{3,2},{4,0},{5,1},{6,7},{7,6},{8,12},{9,13},{10,... | collective-permute-start | bytes 1990664 | tf_op jit(solution)/shard_map/ppermute | solution.py:54
  74.9 17.1 %collective-permute-start.22 = (bf16[2,48,3456]{2,1,0:T(8,128)(2,1)S(1)}, bf16[2,48,3456]{2,1,0:T(8,128)(2,1)}, u32[]{:S(2)}, u32[]{:S(2)}) collective-permute-start(bf16[2,48,3456]{2,1,0:T(8,128)(2,1)S(1)} %pad_maximum_fusion.rest_0_), channel_id=1, source_target_pairs={{0,2},{1,3},{2,0},{3,1},{4,6},{5,7},{6,4},{7,5},{8,10},{9,11},{10,... | collective-permute-start | bytes 1990664 | tf_op jit(solution)/shard_map/ppermute | solution.py:54
  74.9 17.2 %collective-permute-start.23 = (bf16[2,48,3456]{2,1,0:T(8,128)(2,1)S(1)}, bf16[2,48,3456]{2,1,0:T(8,128)(2,1)}, u32[]{:S(2)}, u32[]{:S(2)}) collective-permute-start(bf16[2,48,3456]{2,1,0:T(8,128)(2,1)S(1)} %collective-permute-done.19.rest_1_), channel_id=1, source_target_pairs={{0,2},{1,3},{2,0},{3,1},{4,6},{5,7},{6,4},{7,5},{8,10},{9,11},{10,... | collective-permute-start | bytes 1990664 | tf_op jit(solution)/shard_map/ppermute | solution.py:54
  75.4 17.1 %collective-permute-start.24 = (bf16[2,48,3456]{2,1,0:T(8,128)(2,1)S(1)}, bf16[2,48,3456]{2,1,0:T(8,128)(2,1)}, u32[]{:S(2)}, u32[]{:S(2)}) collective-permute-start(bf16[2,48,3456]{2,1,0:T(8,128)(2,1)S(1)} %collective-permute-done.20.rest_2_), channel_id=1, source_target_pairs={{0,2},{1,3},{2,0},{3,1},{4,6},{5,7},{6,4},{7,5},{8,10},{9,11},{10,... | collective-permute-start | bytes 1990664 | tf_op jit(solution)/shard_map/ppermute | solution.py:54
  75.5 16.0 %collective-permute-start.30 = (bf16[2,48,3456]{2,1,0:T(8,128)(2,1)S(1)}, bf16[2,48,3456]{2,1,0:T(8,128)(2,1)}, u32[]{:S(2)}, u32[]{:S(2)}) collective-permute-start(bf16[2,48,3456]{2,1,0:T(8,128)(2,1)S(1)} %collective-permute-done.29.rest_10_), channel_id=1, source_target_pairs={{0,4},{1,5},{2,3},{3,2},{4,0},{5,1},{6,7},{7,6},{8,12},{9,13},{10,... | collective-permute-start | bytes 1990664 | tf_op jit(solution)/shard_map/ppermute | solution.py:54
  121.2 24.9 %collective-permute-start.35 = (bf16[1,512,768]{2,1,0:T(8,128)(2,1)}, bf16[1,512,768]{2,1,0:T(8,128)(2,1)S(1)}, u32[]{:S(2)}, u32[]{:S(2)}) collective-permute-start(bf16[1,512,768]{2,1,0:T(8,128)(2,1)} %get-tuple-element.66), channel_id=1, source_target_pairs={{0,1},{1,0},{2,3},{3,2},{4,5},{5,4},{6,7},{7,6},{8,9},{9,8},{10,11... | collective-permute-start | bytes 2359304 | tf_op jit(solution)/shard_map/ppermute | solution.py:644
  144.8 20.8 %collective-permute-start.36 = (bf16[1,512,768]{2,1,0:T(8,128)(2,1)}, bf16[1,512,768]{2,1,0:T(8,128)(2,1)S(1)}, u32[]{:S(2)}, u32[]{:S(2)}) collective-permute-start(bf16[1,512,768]{2,1,0:T(8,128)(2,1)} %get-tuple-element.70), channel_id=1, source_target_pairs={{0,1},{1,0},{2,3},{3,2},{4,5},{5,4},{6,7},{7,6},{8,9},{9,8},{10,11... | collective-permute-start | bytes 2359304 | tf_op jit(solution)/shard_map/ppermute | solution.py:647
  164.8 19.3 %collective-permute-start.37 = (bf16[1,512,768]{2,1,0:T(8,128)(2,1)}, bf16[1,512,768]{2,1,0:T(8,128)(2,1)S(1)}, u32[]{:S(2)}, u32[]{:S(2)}) collective-permute-start(bf16[1,512,768]{2,1,0:T(8,128)(2,1)} %get-tuple-element.81), channel_id=1, source_target_pairs={{0,1},{1,0},{2,3},{3,2},{4,5},{5,4},{6,7},{7,6},{8,9},{9,8},{10,11... | collective-permute-start | bytes 2359304 | tf_op jit(solution)/shard_map/ppermute | solution.py:650
  184.1 18.3 %collective-permute-start.38 = (bf16[1,512,768]{2,1,0:T(8,128)(2,1)}, bf16[1,512,768]{2,1,0:T(8,128)(2,1)S(1)}, u32[]{:S(2)}, u32[]{:S(2)}) collective-permute-start(bf16[1,512,768]{2,1,0:T(8,128)(2,1)} %get-tuple-element.87), channel_id=1, source_target_pairs={{0,1},{1,0},{2,3},{3,2},{4,5},{5,4},{6,7},{7,6},{8,9},{9,8},{10,11... | collective-permute-start | bytes 2359304 | tf_op jit(solution)/shard_map/ppermute | solution.py:653
  (49 other events, 527.9 us)

commit v2 on v1

--- a/solution.py
+++ b/solution.py
@@ -435,7 +435,8 @@
     pos, count, info, qkv_ref, p_ref, z_ref, gctx_ref, g1_ref, own_ref, peer_ref, qd_ref, vd_ref, *rest
 ):
     pieces = rest[:count]
-    full_ref, grad_ref, lora_ref, w, dqkv, total, sems = rest[-7:]
+    full_ref, grad_ref, mine_ref, other_ref, w, dqkv, total, sems = rest[-8:]
+    earlier = rest[count : count + 2]
     slots, width = qkv_ref.shape[1], own_ref.shape[1]
     turn, pair = pl.program_id(0), pl.program_id(1)
     half = info[9] ^ turn
@@ -455,6 +456,7 @@
             v2 = qkv_ref[0, rows, pl.ds(2 * width + col, 128)]
             g2 = gctx_ref[0, rows]
             dq = dk = dv = jnp.zeros((size, 128), F32)
+            joined = []
             for e in range(2):
                 probs = p_ref[0, e, rows, :size]
                 dp = mm(g2, v2 * masks[e], NT)
@@ -462,8 +464,16 @@
                 p32 = probs.astype(F32)
                 pd = p32 * dp
                 ds = (pd - p32 * jnp.sum(pd, axis=1, keepdims=True)).astype(BF16)
-                dq = dq + mm(ds, k2 * masks[e])
-                dk = dk + mm(ds, q2 * masks[e], TN)
+                if size == slots:
+                    joined.append(ds)
+                else:
+                    dq = dq + mm(ds, k2 * masks[e])
+                    dk = dk + mm(ds, q2 * masks[e], TN)
+            if joined:
+                ds = jnp.concatenate(joined, axis=1)
+                dq = mm(ds, jnp.concatenate([k2 * masks[0], k2 * masks[1]], axis=0))
+                dk = mm(ds, q2, TN)
+                dk = jnp.where(lax.broadcasted_iota(jnp.int32, (1, 128), 1) < 64, dk[:size], dk[size:])
             dqkv[rows, pl.ds(col, 128)] = dq.astype(BF16)
             dqkv[rows, pl.ds(width + col, 128)] = dk.astype(BF16)
             dqkv[rows, pl.ds(2 * width + col, 128)] = dv.astype(BF16)
@@ -477,16 +487,17 @@
         w[half, model:] = adapter_rows(own_ref, peer_ref, turn, rank)[0]
         part = mm(dqkv[...], w[half], NT)
         lora = 2.0 * mm(z_ref[0], dqkv[...], TN)
-        lora_ref[0, :, :width] = lora[:rank, :width]
-        lora_ref[0, :, width:] = lora[rank:, 2 * width :]
+        lora = jnp.concatenate([lora[:rank, :width], lora[rank:, 2 * width :]], axis=1)
 
         @pl.when(turn == 0)
         def _():
+            mine_ref[...] = lora if pos == 0 else lora + earlier[0][...]
             total[:, :model] = g1_ref[0] + part[:, :model]
             total[:, model:] = part[:, model:]
 
         @pl.when(turn == 1)
         def _():
+            other_ref[...] = lora if pos == 0 else lora + earlier[1][...]
             t = total[:, model:] + part[:, model:]
             tq, tv = split(t[:, :rank] + t[:, rank : 2 * rank]), split(t[:, 2 * rank : 3 * rank] + t[:, 3 * rank :])
             down = jnp.concatenate([qd_ref[...], vd_ref[...]] * 2, axis=0)
@@ -496,7 +507,7 @@
             full_ref[0] = grad_ref[0]
 
 
-def run_bwd(pos, info, qkv, probs, ctx, z, gctx, g1, pieces, small, peer_small, query_down, value_down, full):
+def run_bwd(pos, info, qkv, probs, ctx, z, gctx, g1, pieces, small, peer_small, query_down, value_down, full, earlier=()):
     _, slots, width3 = qkv.shape
     half, model = width3 // 3, g1.shape[2]
     pairs, wide = half // 128, probs.shape[3]
@@ -513,6 +524,8 @@
         pl.BlockSpec(value_down.shape, whole),
     ] + [any_spec() for _ in pieces]
     args = [info, qkv, probs, z, gctx, g1, small, peer_small, query_down, value_down, *pieces]
+    in_specs += [pl.BlockSpec(e.shape, whole) for e in earlier]
+    args += earlier
     aliases = {}
     if full is not None:
         in_specs.append(any_spec())
@@ -523,7 +536,8 @@
         out_shape=(
             jax.ShapeDtypeStruct((4, slots, model), BF16),
             jax.ShapeDtypeStruct((1, slots, model), BF16),
-            jax.ShapeDtypeStruct((2, query_down.shape[0], 2 * half), F32),
+            jax.ShapeDtypeStruct((query_down.shape[0], 2 * half), F32),
+            jax.ShapeDtypeStruct((query_down.shape[0], 2 * half), F32),
         ),
         grid_spec=pltpu.PrefetchScalarGridSpec(
             num_scalar_prefetch=1,
@@ -532,7 +546,8 @@
             out_specs=[
                 pl.BlockSpec((1, slots, model), lambda i, j, info: (info[pos], 0, 0)),
                 pl.BlockSpec((1, slots, model), lambda i, j, info: (0, 0, 0)),
-                pl.BlockSpec((1, query_down.shape[0], 2 * half), lambda i, j, info: (i ^ info[9], 0, 0)),
+                pl.BlockSpec((query_down.shape[0], 2 * half), whole),
+                pl.BlockSpec((query_down.shape[0], 2 * half), whole),
             ],
             scratch_shapes=[
                 pltpu.VMEM((2, model + 4 * query_down.shape[0], width3), BF16),
@@ -646,17 +661,16 @@
     acts, a1, g1_1, gctx1 = run_mid(1, info, tokens, ctx, cotangent, live, wrest, small, peer_small, vec, acts)
     p_a1 = lax.ppermute(a1, "head", SWAP)
     gctx0 = then(gctx0, (p_a0, a1))
-    grads, g0, lora0 = run_bwd(0, info, *first, gctx0, g1_0, *shared, grads)
+    grads, g0, *lora = run_bwd(0, info, *first, gctx0, g1_0, *shared, grads)
     p_g0 = lax.ppermute(g0, "head", SWAP)
     gctx1 = then(gctx1, (p_a1, g0))
-    grads, g1, lora1 = run_bwd(1, info, *second, gctx1, g1_1, *shared, grads)
-    p_g1 = lax.ppermute(then(g1, p_g0), "head", SWAP)
-    lora = sum_over_dp(lora0 + lora1)
-    mine, other = jnp.where(me == 0, lora, lora[::-1])
+    grads, g1, mine, other = run_bwd(1, info, *second, gctx1, g1_1, *shared, grads, lora)
+    received = lax.ppermute(other, "head", SWAP)
+    p_g1 = lax.ppermute(then(g1, (received, p_g0)), "head", SWAP)
+    lora = sum_over_dp(mine + received)
     acts = place(0, info, acts, [p_a0, p_a1])
     grads = place(0, info, grads, [p_g0])
-    p_g1, other = then(p_g1, (acts, grads, lora)), then(other, p_g1)
-    lora = mine + lax.ppermute(other, "head", SWAP)
+    p_g1 = then(p_g1, (acts, grads, lora))
     grads = place(1, info, grads, [p_g1])
     return acts, grads, lora[:, :half], lora[:, half:]
 

time: 208 us -> 206 us (level)
    ppermute x1, waiting for transfers between devices: 2.12 us -> 0.01 us  [shards(): p_g0 = lax.ppermute(g0, 'head', SWAP)]
  transfers between devices with their start and end apart: 44 -> 44, of which waited for: 20 -> 19; matrix products, arithmetic and copies ran while one was open for 1% -> 2% of each run, Pallas kernels for 47% -> 46%
where the time goes in v2:
time: 206 us; the launch traced here: 205 us
  Pallas kernels  120 us (58%)
  waiting for transfers between devices  43.2 us (21%)
  starting transfers between devices  35.5 us (17%)
  local copies, waits for them, and re-layouts  2.53 us (1%)
  other arithmetic  2.51 us (1%)
    pallas_call x2, Pallas kernels, run_mid(): pl.pallas_call(functools.partial(mid_kernel, pos, len(pieces)), out_shape...  45.5 us
    ppermute x34, waiting for transfers between devices, permuter(): return lambda a, which: lax.ppermute(a, ('dp', 'head'), tables[which])  33.9 us
    pallas_call x2, Pallas kernels, run_fwd(): pl.pallas_call(functools.partial(fwd_kernel, pos, len(pieces)), out_shape...  33.8 us
    pallas_call x2, Pallas kernels, run_bwd(): pl.pallas_call(functools.partial(bwd_kernel, pos, len(pieces)), out_shape...  33.2 us
    ppermute x34, starting transfers between devices, permuter(): return lambda a, which: lax.ppermute(a, ('dp', 'head'), tables[which])  21.4 us
    ppermute x4, starting transfers between devices, sum_over_dp(): a = a + lax.ppermute(a, 'dp', [(i, i ^ bit) for i in range(size)])  7.02 us
    ppermute x4, waiting for transfers between devices, sum_over_dp(): a = a + lax.ppermute(a, 'dp', [(i, i ^ bit) for i in range(size)])  6.47 us
    pallas_call x3, Pallas kernels, place(): pl.pallas_call(functools.partial(place_kernel, pos), out_shape=jax.ShapeD...  4.56 us
  transfers between devices with their start and end apart: 44, of which 19 were waited for; matrix products, arithmetic and copies ran while one was open for 2% of the time, Pallas kernels for 46%

profile of v2, /device:TPU:0, one launch (start us, length us, event | category | flops | bytes accessed | tf_op | source)
XLA Modules:
  0.0 205.4 jit_solution(15633161894083838642)
XLA Ops:
  2.1 3.0 %collective-permute-start.1 = (bf16[48,1152]{1,0:T(8,128)(2,1)}, bf16[48,1152]{1,0:T(8,128)(2,1)S(1)}, u32[]{:S(2)}, u32[]{:S(2)}) collective-permute-start(bf16[48,1152]{1,0:T(8,128)(2,1)} %pack.1), channel_id=1, source_target_pairs={{0,8},{1,9},{2,10},{3,11},{4,12},{5,13},{6,14},{7,15},{8,16},{9,17... | collective-permute-start | bytes 331784 | tf_op jit(solution)/shard_map/ppermute | solution.py:54
  5.7 4.7 %collective-permute-done.1 = bf16[48,1152]{1,0:T(8,128)(2,1)S(1)} collective-permute-done((bf16[48,1152]{1,0:T(8,128)(2,1)}, bf16[48,1152]{1,0:T(8,128)(2,1)S(1)}, u32[]{:S(2)}, u32[]{:S(2)}) %collective-permute-start.1) | collective-permute-done | bytes 110624 | tf_op jit(solution)/shard_map/ppermute | solution.py:54
  10.4 1.9 prepare.1
  15.2 2.5 %collective-permute-done.9 = bf16[48,1152]{1,0:T(8,128)(2,1)S(1)} collective-permute-done((bf16[48,1152]{1,0:T(8,128)(2,1)S(1)}, bf16[48,1152]{1,0:T(8,128)(2,1)S(1)}, u32[]{:S(2)}, u32[]{:S(2)}) %collective-permute-start.9) | collective-permute-done | bytes 110624 | tf_op jit(solution)/shard_map/ppermute | solution.py:54
  17.9 1.8 collective-permute-start.3
  19.6 6.8 %collective-permute-done.10 = bf16[48,1152]{1,0:T(8,128)(2,1)S(1)} collective-permute-done((bf16[48,1152]{1,0:T(8,128)(2,1)S(1)}, bf16[48,1152]{1,0:T(8,128)(2,1)S(1)}, u32[]{:S(2)}, u32[]{:S(2)}) %collective-permute-start.10) | collective-permute-done | bytes 110624 | tf_op jit(solution)/shard_map/ppermute | solution.py:54
  28.1 1.6 collective-permute-start.12
  30.2 3.3 %collective-permute-done.2.rest_1_ = bf16[2,48,1152]{2,1,0:T(8,128)(2,1)S(1)} collective-permute-done((bf16[2,48,1152]{2,1,0:T(8,128)(2,1)S(1)}, bf16[2,48,1152]{2,1,0:T(8,128)(2,1)S(1)}, u32[]{:S(2)}, u32[]{:S(2)}) %collective-permute-start.2) | collective-permute-done | bytes 221216 | tf_op jit(solution)/shard_map/ppermute | solution.py:54
  33.6 1.6 collective-permute-start.4
  41.4 1.6 collective-permute-done.13.rest_11_
  43.0 6.7 %collective-permute-done.27 = bf16[48,3456]{1,0:T(8,128)(2,1)S(1)} collective-permute-done((bf16[48,3456]{1,0:T(8,128)(2,1)S(1)}, bf16[48,3456]{1,0:T(8,128)(2,1)S(1)}, u32[]{:S(2)}, u32[]{:S(2)}) %collective-permute-start.27) | collective-permute-done | bytes 331808 | tf_op jit(solution)/shard_map/ppermute | solution.py:54
  53.4 19.0 %attention_forward.2 = (bf16[2,512,1152]{2,1,0:T(8,128)(2,1)}, bf16[2,6,512,512]{3,2,1,0:T(8,128)(2,1)}, bf16[1,512,768]{2,1,0:T(8,128)(2,1)}, bf16[1,512,16]{2,1,0:T(8,128)(2,1)}) custom-call(s32[10]{0:T(128)} %get-tuple-element.52.info, bf16[4,512,768]{2,1,0:T(8,128)(2,1)} %x_ref.7, f32[22,384]{1,0:T(8,128)} %get-tuple-element.50.own_ref, ...), custom_call_target="tpu_custom_call" | custom-call | flops 12000000000 | bytes 8388608 | tf_op jit(solution)/shard_map/attention_forward/pallas_call | solution.py:266
  76.5 14.8 %attention_forward.3 = (bf16[2,512,1152]{2,1,0:T(8,128)(2,1)}, bf16[2,6,512,256]{3,2,1,0:T(8,128)(2,1)}, bf16[1,512,768]{2,1,0:T(8,128)(2,1)}, bf16[1,512,16]{2,1,0:T(8,128)(2,1)}) custom-call(s32[10]{0:T(128)} %get-tuple-element.52.info, bf16[4,512,768]{2,1,0:T(8,128)(2,1)} %x_ref.7, f32[22,384]{1,0:T(8,128)} %get-tuple-element.50.own_ref, ...), custom_call_target="tpu_custom_call" | custom-call | flops 12000000000 | bytes 8388608 | tf_op jit(solution)/shard_map/attention_forward/pallas_call | solution.py:266
  93.8 1.7 collective-permute-done.31.rest_12_
  95.5 1.9 collective-permute-done.32.rest_13_
  98.6 22.7 %feed_forward.2 = (bf16[4,512,768]{2,1,0:T(8,128)(2,1)}, bf16[1,512,768]{2,1,0:T(8,128)(2,1)}, f32[1,512,768]{2,1,0:T(8,128)}, bf16[1,512,768]{2,1,0:T(8,128)(2,1)}) custom-call(s32[10]{0:T(128)} %get-tuple-element.52.info, bf16[4,512,768]{2,1,0:T(8,128)(2,1)} %x_ref.7, bf16[1,512,768]{2,1,0:T(8,128)(2,1)} %get-tuple-element.54.ctx_ref, ...), custom_call_target="tpu_custom_call" | custom-call | flops 24000000000 | bytes 8388608 | tf_op jit(solution)/shard_map/feed_forward/pallas_call | solution.py:401
  122.2 22.8 %feed_forward.3 = (bf16[4,512,768]{2,1,0:T(8,128)(2,1)}, bf16[1,512,768]{2,1,0:T(8,128)(2,1)}, f32[1,512,768]{2,1,0:T(8,128)}, bf16[1,512,768]{2,1,0:T(8,128)(2,1)}) custom-call(s32[10]{0:T(128)} %get-tuple-element.52.info, bf16[4,512,768]{2,1,0:T(8,128)(2,1)} %x_ref.7, ...), custom_call_target="tpu_custom_call", output_to_operand_aliasing={{0}: (24, {})} | custom-call | flops 24000000000 | bytes 8388608 | tf_op jit(solution)/shard_map/feed_forward/pallas_call | solution.py:401
  146.4 17.6 %attention_backward.2 = (bf16[4,512,768]{2,1,0:T(8,128)(2,1)}, bf16[1,512,768]{2,1,0:T(8,128)(2,1)}, f32[8,768]{1,0:T(8,128)}, f32[8,768]{1,0:T(8,128)}) custom-call(s32[10]{0:T(128)} %get-tuple-element.52.info, bf16[2,512,1152]{2,1,0:T(8,128)(2,1)} %get-tuple-element.76.qkv_ref, bf16[2,6,512,512]{3,2,1,0:T(8,128)(2,1)} %get-tuple-element.77.p_ref, ...), custom_call_target="tpu_custom_call" | custom-call | flops 16000000000 | bytes 8388608 | tf_op jit(solution)/shard_map/attention_backward/pallas_call | solution.py:534
  164.8 15.6 %attention_backward.3 = (bf16[4,512,768]{2,1,0:T(8,128)(2,1)}, bf16[1,512,768]{2,1,0:T(8,128)(2,1)}, f32[8,768]{1,0:T(8,128)}, f32[8,768]{1,0:T(8,128)}) custom-call(s32[10]{0:T(128)} %get-tuple-element.52.info, bf16[2,512,1152]{2,1,0:T(8,128)(2,1)} %get-tuple-element.72.qkv_ref, ...), custom_call_target="tpu_custom_call", output_to_operand_aliasing={{0}: (28, {})} | custom-call | flops 16000000000 | bytes 8388608 | tf_op jit(solution)/shard_map/attention_backward/pallas_call | solution.py:534
  181.7 2.8 %collective-permute-done.38 = f32[8,768]{1,0:T(8,128)S(1)} collective-permute-done((f32[8,768]{1,0:T(8,128)}, f32[8,768]{1,0:T(8,128)S(1)}, u32[]{:S(2)}, u32[]{:S(2)}) %collective-permute-start.38) | collective-permute-done | bytes 24608 | tf_op jit(solution)/shard_map/ppermute | solution.py:668
  188.7 2.8 %collective-permute-done.41 = f32[8,768]{1,0:T(8,128)S(1)} collective-permute-done((f32[8,768]{1,0:T(8,128)S(1)}, f32[8,768]{1,0:T(8,128)S(1)}, u32[]{:S(2)}, u32[]{:S(2)}) %collective-permute-start.41) | collective-permute-done | bytes 24608 | tf_op jit(solution)/shard_map/ppermute | solution.py:602
  193.0 2.3 %collective-permute-done.42 = f32[8,768]{1,0:T(8,128)S(1)} collective-permute-done((f32[8,768]{1,0:T(8,128)S(1)}, f32[8,768]{1,0:T(8,128)S(1)}, u32[]{:S(2)}, u32[]{:S(2)}) %collective-permute-start.42) | collective-permute-done | bytes 24608 | tf_op jit(solution)/shard_map/ppermute | solution.py:602
  195.4 4.5 %collective-permute-start.43 = (f32[8,768]{1,0:T(8,128)S(1)}, f32[8,768]{1,0:T(8,128)S(1)}, u32[]{:S(2)}, u32[]{:S(2)}) collective-permute-start(f32[8,768]{1,0:T(8,128)S(1)} %add.18), channel_id=1, source_target_pairs={{0,16},{2,18},{4,20},{6,22},{8,24},{10,26},{12,28},{14,30},{16,0},... | collective-permute-start | bytes 73736 | tf_op jit(solution)/shard_map/ppermute | solution.py:602
  199.9 1.7 place.3
  (144 shorter events, 38.3 us)
Async XLA Ops:
  2.1 8.3 %collective-permute-start.1 = (bf16[48,1152]{1,0:T(8,128)(2,1)}, bf16[48,1152]{1,0:T(8,128)(2,1)S(1)}, u32[]{:S(2)}, u32[]{:S(2)}) collective-permute-start(bf16[48,1152]{1,0:T(8,128)(2,1)} %pack.1), channel_id=1, source_target_pairs={{0,8},{1,9},{2,10},{3,11},{4,12},{5,13},{6,14},{7,15},{8,16},{9,17... | collective-permute-start | bytes 331784 | tf_op jit(solution)/shard_map/ppermute | solution.py:54
  12.3 15.6 %collective-permute-start.18 = (bf16[48,3456]{1,0:T(8,128)(2,1)}, bf16[48,3456]{1,0:T(8,128)(2,1)S(1)}, u32[]{:S(2)}, u32[]{:S(2)}) collective-permute-start(bf16[48,3456]{1,0:T(8,128)(2,1)} %get-tuple-element.57), channel_id=1, source_target_pairs={{0,8},{1,9},{2,10},{3,11},{4,12},{5,13},{6,14},{7,15},{8,16},{9,17... | collective-permute-start | bytes 995336 | tf_op jit(solution)/shard_map/ppermute | solution.py:54
  13.7 14.3 %collective-permute-start = (f32[22,384]{1,0:T(8,128)}, f32[22,384]{1,0:T(8,128)S(1)}, u32[]{:S(2)}, u32[]{:S(2)}) collective-permute-start(f32[22,384]{1,0:T(8,128)} %get-tuple-element.50.own_ref), channel_id=1, source_target_pairs={{0,1},{1,0},{2,3},{3,2},{4,5},{5,4},{6,7},{7,6},{8,9},{9,8},{10,11... | collective-permute-start | bytes 101384 | tf_op jit(solution)/shard_map/ppermute | solution.py:624
  17.7 8.7 %collective-permute-start.10 = (bf16[48,1152]{1,0:T(8,128)(2,1)S(1)}, bf16[48,1152]{1,0:T(8,128)(2,1)S(1)}, u32[]{:S(2)}, u32[]{:S(2)}) collective-permute-start(bf16[48,1152]{1,0:T(8,128)(2,1)S(1)} %collective-permute-done.9), channel_id=1, source_target_pairs={{0,8},{1,9},{2,10},{3,11},{4,12},{5,13},{6,14},{7,15},{8,16},{9,17... | collective-permute-start | bytes 331784 | tf_op jit(solution)/shard_map/ppermute | solution.py:54
  17.8 10.3 %collective-permute-start.5 = (bf16[2,48,1152]{2,1,0:T(8,128)(2,1)S(1)}, bf16[2,48,1152]{2,1,0:T(8,128)(2,1)S(1)}, u32[]{:S(2)}, u32[]{:S(2)}) collective-permute-start(bf16[2,48,1152]{2,1,0:T(8,128)(2,1)S(1)} %pad_maximum_fusion.2.rest_0_), channel_id=1, source_target_pairs={{0,2},{1,3},{2,0},{3,1},{4,6},{5,7},{6,4},{7,5},{8,10},{9,11},{10,... | collective-permute-start | bytes 663560 | tf_op jit(solution)/shard_map/ppermute | solution.py:54
  17.9 11.8 %collective-permute-start.3 = (bf16[2,48,1152]{2,1,0:T(8,128)(2,1)S(1)}, bf16[2,48,1152]{2,1,0:T(8,128)(2,1)S(1)}, u32[]{:S(2)}, u32[]{:S(2)}) collective-permute-start(bf16[2,48,1152]{2,1,0:T(8,128)(2,1)S(1)} %pad_maximum_fusion.2.rest_0_), channel_id=1, source_target_pairs={{0,1},{1,0},{2,6},{3,7},{4,5},{5,4},{6,2},{7,3},{8,9},{9,8},{10,14... | collective-permute-start | bytes 663560 | tf_op jit(solution)/shard_map/ppermute | solution.py:54
  27.9 10.7 %collective-permute-start.26 = (bf16[48,3456]{1,0:T(8,128)(2,1)S(1)}, bf16[48,3456]{1,0:T(8,128)(2,1)S(1)}, u32[]{:S(2)}, u32[]{:S(2)}) collective-permute-start(bf16[48,3456]{1,0:T(8,128)(2,1)S(1)} %collective-permute-done.18), channel_id=1, source_target_pairs={{0,8},{1,9},{2,10},{3,11},{4,12},{5,13},{6,14},{7,15},{8,16},{9,17... | collective-permute-start | bytes 995336 | tf_op jit(solution)/shard_map/ppermute | solution.py:54
  38.6 11.1 %collective-permute-start.27 = (bf16[48,3456]{1,0:T(8,128)(2,1)S(1)}, bf16[48,3456]{1,0:T(8,128)(2,1)S(1)}, u32[]{:S(2)}, u32[]{:S(2)}) collective-permute-start(bf16[48,3456]{1,0:T(8,128)(2,1)S(1)} %collective-permute-done.26), channel_id=1, source_target_pairs={{0,8},{1,9},{2,10},{3,11},{4,12},{5,13},{6,14},{7,15},{8,16},{9,17... | collective-permute-start | bytes 995336 | tf_op jit(solution)/shard_map/ppermute | solution.py:54
  39.7 12.3 %collective-permute-start.19 = (bf16[2,48,3456]{2,1,0:T(8,128)(2,1)S(1)}, bf16[2,48,3456]{2,1,0:T(8,128)(2,1)S(1)}, u32[]{:S(2)}, u32[]{:S(2)}) collective-permute-start(bf16[2,48,3456]{2,1,0:T(8,128)(2,1)S(1)} %pad_maximum_fusion.rest_0_), channel_id=1, source_target_pairs={{0,4},{1,5},{2,3},{3,2},{4,0},{5,1},{6,7},{7,6},{8,12},{9,13},{10,... | collective-permute-start | bytes 1990664 | tf_op jit(solution)/shard_map/ppermute | solution.py:54
  40.9 9.0 %collective-permute-start.16 = (bf16[2,48,1152]{2,1,0:T(8,128)(2,1)S(1)}, bf16[2,48,1152]{2,1,0:T(8,128)(2,1)S(1)}, u32[]{:S(2)}, u32[]{:S(2)}) collective-permute-start(bf16[2,48,1152]{2,1,0:T(8,128)(2,1)S(1)} %collective-permute-done.12.rest_10_), channel_id=1, source_target_pairs={{0,2},{1,3},{2,0},{3,1},{4,6},{5,7},{6,4},{7,5},{8,10},{9,11},{10,... | collective-permute-start | bytes 663560 | tf_op jit(solution)/shard_map/ppermute | solution.py:54
  40.9 9.5 %collective-permute-start.15 = (bf16[2,48,1152]{2,1,0:T(8,128)(2,1)S(1)}, bf16[2,48,1152]{2,1,0:T(8,128)(2,1)S(1)}, u32[]{:S(2)}, u32[]{:S(2)}) collective-permute-start(bf16[2,48,1152]{2,1,0:T(8,128)(2,1)S(1)} %collective-permute-done.11.rest_9_), channel_id=1, source_target_pairs={{0,2},{1,3},{2,0},{3,1},{4,6},{5,7},{6,4},{7,5},{8,10},{9,11},{10,... | collective-permute-start | bytes 663560 | tf_op jit(solution)/shard_map/ppermute | solution.py:54
  43.0 9.5 %collective-permute-start.8 = (bf16[2,48,1152]{2,1,0:T(8,128)(2,1)S(1)}, bf16[2,48,1152]{2,1,0:T(8,128)(2,1)S(1)}, u32[]{:S(2)}, u32[]{:S(2)}) collective-permute-start(bf16[2,48,1152]{2,1,0:T(8,128)(2,1)S(1)} %collective-permute-done.4.rest_3_), channel_id=1, source_target_pairs={{0,2},{1,3},{2,0},{3,1},{4,6},{5,7},{6,4},{7,5},{8,10},{9,11},{10,... | collective-permute-start | bytes 663560 | tf_op jit(solution)/shard_map/ppermute | solution.py:54
  49.9 23.8 %collective-permute-start.20 = (bf16[2,48,3456]{2,1,0:T(8,128)(2,1)S(1)}, bf16[2,48,3456]{2,1,0:T(8,128)(2,1)S(1)}, u32[]{:S(2)}, u32[]{:S(2)}) collective-permute-start(bf16[2,48,3456]{2,1,0:T(8,128)(2,1)S(1)} %pad_maximum_fusion.rest_0_), channel_id=1, source_target_pairs={{0,1},{1,0},{2,6},{3,7},{4,5},{5,4},{6,2},{7,3},{8,9},{9,8},{10,14... | collective-permute-start | bytes 1990664 | tf_op jit(solution)/shard_map/ppermute | solution.py:54
  50.4 23.2 %collective-permute-start.29 = (bf16[2,48,3456]{2,1,0:T(8,128)(2,1)S(1)}, bf16[2,48,3456]{2,1,0:T(8,128)(2,1)}, u32[]{:S(2)}, u32[]{:S(2)}) collective-permute-start(bf16[2,48,3456]{2,1,0:T(8,128)(2,1)S(1)} %pad_maximum_fusion.1.rest_8_), channel_id=1, source_target_pairs={{0,1},{1,0},{2,6},{3,7},{4,5},{5,4},{6,2},{7,3},{8,9},{9,8},{10,14... | collective-permute-start | bytes 1990664 | tf_op jit(solution)/shard_map/ppermute | solution.py:54
  52.0 23.0 %collective-permute-start.21 = (bf16[2,48,3456]{2,1,0:T(8,128)(2,1)S(1)}, bf16[2,48,3456]{2,1,0:T(8,128)(2,1)}, u32[]{:S(2)}, u32[]{:S(2)}) collective-permute-start(bf16[2,48,3456]{2,1,0:T(8,128)(2,1)S(1)} %collective-permute-done.19.rest_1_), channel_id=1, source_target_pairs={{0,1},{1,0},{2,6},{3,7},{4,5},{5,4},{6,2},{7,3},{8,9},{9,8},{10,14... | collective-permute-start | bytes 1990664 | tf_op jit(solution)/shard_map/ppermute | solution.py:54
  72.4 19.0 %collective-permute-start.28 = (bf16[2,48,3456]{2,1,0:T(8,128)(2,1)S(1)}, bf16[2,48,3456]{2,1,0:T(8,128)(2,1)S(1)}, u32[]{:S(2)}, u32[]{:S(2)}) collective-permute-start(bf16[2,48,3456]{2,1,0:T(8,128)(2,1)S(1)} %pad_maximum_fusion.1.rest_8_), channel_id=1, source_target_pairs={{0,4},{1,5},{2,3},{3,2},{4,0},{5,1},{6,7},{7,6},{8,12},{9,13},{10,... | collective-permute-start | bytes 1990664 | tf_op jit(solution)/shard_map/ppermute | solution.py:54
  74.9 17.1 %collective-permute-start.22 = (bf16[2,48,3456]{2,1,0:T(8,128)(2,1)S(1)}, bf16[2,48,3456]{2,1,0:T(8,128)(2,1)}, u32[]{:S(2)}, u32[]{:S(2)}) collective-permute-start(bf16[2,48,3456]{2,1,0:T(8,128)(2,1)S(1)} %pad_maximum_fusion.rest_0_), channel_id=1, source_target_pairs={{0,2},{1,3},{2,0},{3,1},{4,6},{5,7},{6,4},{7,5},{8,10},{9,11},{10,... | collective-permute-start | bytes 1990664 | tf_op jit(solution)/shard_map/ppermute | solution.py:54
  74.9 17.2 %collective-permute-start.23 = (bf16[2,48,3456]{2,1,0:T(8,128)(2,1)S(1)}, bf16[2,48,3456]{2,1,0:T(8,128)(2,1)}, u32[]{:S(2)}, u32[]{:S(2)}) collective-permute-start(bf16[2,48,3456]{2,1,0:T(8,128)(2,1)S(1)} %collective-permute-done.19.rest_1_), channel_id=1, source_target_pairs={{0,2},{1,3},{2,0},{3,1},{4,6},{5,7},{6,4},{7,5},{8,10},{9,11},{10,... | collective-permute-start | bytes 1990664 | tf_op jit(solution)/shard_map/ppermute | solution.py:54
  75.4 17.1 %collective-permute-start.24 = (bf16[2,48,3456]{2,1,0:T(8,128)(2,1)S(1)}, bf16[2,48,3456]{2,1,0:T(8,128)(2,1)}, u32[]{:S(2)}, u32[]{:S(2)}) collective-permute-start(bf16[2,48,3456]{2,1,0:T(8,128)(2,1)S(1)} %collective-permute-done.20.rest_2_), channel_id=1, source_target_pairs={{0,2},{1,3},{2,0},{3,1},{4,6},{5,7},{6,4},{7,5},{8,10},{9,11},{10,... | collective-permute-start | bytes 1990664 | tf_op jit(solution)/shard_map/ppermute | solution.py:54
  75.5 16.0 %collective-permute-start.30 = (bf16[2,48,3456]{2,1,0:T(8,128)(2,1)}, bf16[2,48,3456]{2,1,0:T(8,128)(2,1)}, u32[]{:S(2)}, u32[]{:S(2)}) collective-permute-start(bf16[2,48,3456]{2,1,0:T(8,128)(2,1)} %collective-permute-done.29.rest_10_), channel_id=1, source_target_pairs={{0,4},{1,5},{2,3},{3,2},{4,0},{5,1},{6,7},{7,6},{8,12},{9,13},{10,... | collective-permute-start | bytes 1990664 | tf_op jit(solution)/shard_map/ppermute | solution.py:54
  121.4 25.0 %collective-permute-start.35 = (bf16[1,512,768]{2,1,0:T(8,128)(2,1)}, bf16[1,512,768]{2,1,0:T(8,128)(2,1)S(1)}, u32[]{:S(2)}, u32[]{:S(2)}) collective-permute-start(bf16[1,512,768]{2,1,0:T(8,128)(2,1)} %get-tuple-element.67), channel_id=1, source_target_pairs={{0,1},{1,0},{2,3},{3,2},{4,5},{5,4},{6,7},{7,6},{8,9},{9,8},{10,11... | collective-permute-start | bytes 2359304 | tf_op jit(solution)/shard_map/ppermute | solution.py:659
  145.0 19.9 %collective-permute-start.36 = (bf16[1,512,768]{2,1,0:T(8,128)(2,1)}, bf16[1,512,768]{2,1,0:T(8,128)(2,1)S(1)}, u32[]{:S(2)}, u32[]{:S(2)}) collective-permute-start(bf16[1,512,768]{2,1,0:T(8,128)(2,1)} %get-tuple-element.71), channel_id=1, source_target_pairs={{0,1},{1,0},{2,3},{3,2},{4,5},{5,4},{6,7},{7,6},{8,9},{9,8},{10,11... | collective-permute-start | bytes 2359304 | tf_op jit(solution)/shard_map/ppermute | solution.py:662
  164.0 20.5 %collective-permute-start.37 = (bf16[1,512,768]{2,1,0:T(8,128)(2,1)}, bf16[1,512,768]{2,1,0:T(8,128)(2,1)S(1)}, u32[]{:S(2)}, u32[]{:S(2)}) collective-permute-start(bf16[1,512,768]{2,1,0:T(8,128)(2,1)} %get-tuple-element.82), channel_id=1, source_target_pairs={{0,1},{1,0},{2,3},{3,2},{4,5},{5,4},{6,7},{7,6},{8,9},{9,8},{10,11... | collective-permute-start | bytes 2359304 | tf_op jit(solution)/shard_map/ppermute | solution.py:665
  184.5 19.3 %collective-permute-start.39 = (bf16[1,512,768]{2,1,0:T(8,128)(2,1)}, bf16[1,512,768]{2,1,0:T(8,128)(2,1)S(1)}, u32[]{:S(2)}, u32[]{:S(2)}) collective-permute-start(bf16[1,512,768]{2,1,0:T(8,128)(2,1)} %get-tuple-element.91), channel_id=1, source_target_pairs={{0,1},{1,0},{2,3},{3,2},{4,5},{5,4},{6,7},{7,6},{8,9},{9,8},{10,11... | collective-permute-start | bytes 2359304 | tf_op jit(solution)/shard_map/ppermute | solution.py:669
  (49 other events, 524.9 us)

commit v3 on v2

--- a/solution.py
+++ b/solution.py
@@ -657,16 +657,15 @@
     ctx = then(first[2], second[2])
     acts, a0, g1_0, gctx0 = run_mid(0, info, tokens, ctx, cotangent, live, wrest, small, peer_small, vec, acts)
     p_a0 = lax.ppermute(a0, "head", SWAP)
-    ctx = then(second[2], a0)
+    grads, g0, *lora = run_bwd(0, info, *first, gctx0, g1_0, *shared, grads)
+    p_g0 = lax.ppermute(g0, "head", SWAP)
+    ctx = then(second[2], (p_a0, g0))
     acts, a1, g1_1, gctx1 = run_mid(1, info, tokens, ctx, cotangent, live, wrest, small, peer_small, vec, acts)
     p_a1 = lax.ppermute(a1, "head", SWAP)
-    gctx0 = then(gctx0, (p_a0, a1))
-    grads, g0, *lora = run_bwd(0, info, *first, gctx0, g1_0, *shared, grads)
-    p_g0 = lax.ppermute(g0, "head", SWAP)
-    gctx1 = then(gctx1, (p_a1, g0))
+    gctx1 = then(gctx1, (p_g0, a1))
     grads, g1, mine, other = run_bwd(1, info, *second, gctx1, g1_1, *shared, grads, lora)
     received = lax.ppermute(other, "head", SWAP)
-    p_g1 = lax.ppermute(then(g1, (received, p_g0)), "head", SWAP)
+    p_g1 = lax.ppermute(then(g1, (received, p_a1)), "head", SWAP)
     lora = sum_over_dp(mine + received)
     acts = place(0, info, acts, [p_a0, p_a1])
     grads = place(0, info, grads, [p_g0])

time: 206 us -> 206 us (level)
  transfers between devices with their start and end apart: 44 -> 44, of which waited for: 19 -> 20; matrix products, arithmetic and copies ran while one was open for 2% -> 2% of each run, Pallas kernels for 46% -> 46%
where the time goes in v3:
time: 206 us; the launch traced here: 205 us
  Pallas kernels  120 us (58%)
  waiting for transfers between devices  42.9 us (21%)
  starting transfers between devices  35.7 us (17%)
  local copies, waits for them, and re-layouts  2.88 us (1%)
  other arithmetic  2.56 us (1%)
    pallas_call x2, Pallas kernels, run_mid(): pl.pallas_call(functools.partial(mid_kernel, pos, len(pieces)), out_shape...  45.3 us
    pallas_call x2, Pallas kernels, run_fwd(): pl.pallas_call(functools.partial(fwd_kernel, pos, len(pieces)), out_shape...  33.8 us
    ppermute x34, waiting for transfers between devices, permuter(): return lambda a, which: lax.ppermute(a, ('dp', 'head'), tables[which])  33.3 us
    pallas_call x2, Pallas kernels, run_bwd(): pl.pallas_call(functools.partial(bwd_kernel, pos, len(pieces)), out_shape...  32.9 us
    ppermute x34, starting transfers between devices, permuter(): return lambda a, which: lax.ppermute(a, ('dp', 'head'), tables[which])  21.4 us
    ppermute x4, starting transfers between devices, sum_over_dp(): a = a + lax.ppermute(a, 'dp', [(i, i ^ bit) for i in range(size)])  7.29 us
    ppermute x4, waiting for transfers between devices, sum_over_dp(): a = a + lax.ppermute(a, 'dp', [(i, i ^ bit) for i in range(size)])  6.61 us
    pallas_call x3, Pallas kernels, place(): pl.pallas_call(functools.partial(place_kernel, pos), out_shape=jax.ShapeD...  4.56 us
  transfers between devices with their start and end apart: 44, of which 20 were waited for; matrix products, arithmetic and copies ran while one was open for 2% of the time, Pallas kernels for 46%

profile of v3, /device:TPU:0, one launch (start us, length us, event | category | flops | bytes accessed | tf_op | source)
XLA Modules:
  0.0 205.2 jit_solution(16766276275792937779)
XLA Ops:
  2.1 3.0 %collective-permute-start.1 = (bf16[48,1152]{1,0:T(8,128)(2,1)}, bf16[48,1152]{1,0:T(8,128)(2,1)S(1)}, u32[]{:S(2)}, u32[]{:S(2)}) collective-permute-start(bf16[48,1152]{1,0:T(8,128)(2,1)} %pack.1), channel_id=1, source_target_pairs={{0,8},{1,9},{2,10},{3,11},{4,12},{5,13},{6,14},{7,15},{8,16},{9,17... | collective-permute-start | bytes 331784 | tf_op jit(solution)/shard_map/ppermute | solution.py:54
  5.8 4.7 %collective-permute-done.1 = bf16[48,1152]{1,0:T(8,128)(2,1)S(1)} collective-permute-done((bf16[48,1152]{1,0:T(8,128)(2,1)}, bf16[48,1152]{1,0:T(8,128)(2,1)S(1)}, u32[]{:S(2)}, u32[]{:S(2)}) %collective-permute-start.1) | collective-permute-done | bytes 110624 | tf_op jit(solution)/shard_map/ppermute | solution.py:54
  10.4 1.9 prepare.1
  15.2 2.5 %collective-permute-done.9 = bf16[48,1152]{1,0:T(8,128)(2,1)S(1)} collective-permute-done((bf16[48,1152]{1,0:T(8,128)(2,1)S(1)}, bf16[48,1152]{1,0:T(8,128)(2,1)S(1)}, u32[]{:S(2)}, u32[]{:S(2)}) %collective-permute-start.9) | collective-permute-done | bytes 110624 | tf_op jit(solution)/shard_map/ppermute | solution.py:54
  17.9 1.8 collective-permute-start.3
  19.6 6.8 %collective-permute-done.10 = bf16[48,1152]{1,0:T(8,128)(2,1)S(1)} collective-permute-done((bf16[48,1152]{1,0:T(8,128)(2,1)S(1)}, bf16[48,1152]{1,0:T(8,128)(2,1)S(1)}, u32[]{:S(2)}, u32[]{:S(2)}) %collective-permute-start.10) | collective-permute-done | bytes 110624 | tf_op jit(solution)/shard_map/ppermute | solution.py:54
  28.1 1.6 collective-permute-start.12
  30.2 3.3 %collective-permute-done.2.rest_1_ = bf16[2,48,1152]{2,1,0:T(8,128)(2,1)S(1)} collective-permute-done((bf16[2,48,1152]{2,1,0:T(8,128)(2,1)S(1)}, bf16[2,48,1152]{2,1,0:T(8,128)(2,1)S(1)}, u32[]{:S(2)}, u32[]{:S(2)}) %collective-permute-start.2) | collective-permute-done | bytes 221216 | tf_op jit(solution)/shard_map/ppermute | solution.py:54
  33.6 1.6 collective-permute-start.4
  41.4 1.6 collective-permute-done.13.rest_11_
  43.0 6.7 %collective-permute-done.27 = bf16[48,3456]{1,0:T(8,128)(2,1)S(1)} collective-permute-done((bf16[48,3456]{1,0:T(8,128)(2,1)S(1)}, bf16[48,3456]{1,0:T(8,128)(2,1)S(1)}, u32[]{:S(2)}, u32[]{:S(2)}) %collective-permute-start.27) | collective-permute-done | bytes 331808 | tf_op jit(solution)/shard_map/ppermute | solution.py:54
  53.4 18.9 %attention_forward.2 = (bf16[2,512,1152]{2,1,0:T(8,128)(2,1)}, bf16[2,6,512,512]{3,2,1,0:T(8,128)(2,1)}, bf16[1,512,768]{2,1,0:T(8,128)(2,1)}, bf16[1,512,16]{2,1,0:T(8,128)(2,1)}) custom-call(s32[10]{0:T(128)} %get-tuple-element.51.info, bf16[4,512,768]{2,1,0:T(8,128)(2,1)} %x_ref.7, f32[22,384]{1,0:T(8,128)} %get-tuple-element.49.own_ref, ...), custom_call_target="tpu_custom_call" | custom-call | flops 12000000000 | bytes 8388608 | tf_op jit(solution)/shard_map/attention_forward/pallas_call | solution.py:266
  76.5 14.8 %attention_forward.3 = (bf16[2,512,1152]{2,1,0:T(8,128)(2,1)}, bf16[2,6,512,256]{3,2,1,0:T(8,128)(2,1)}, bf16[1,512,768]{2,1,0:T(8,128)(2,1)}, bf16[1,512,16]{2,1,0:T(8,128)(2,1)}) custom-call(s32[10]{0:T(128)} %get-tuple-element.51.info, bf16[4,512,768]{2,1,0:T(8,128)(2,1)} %x_ref.7, f32[22,384]{1,0:T(8,128)} %get-tuple-element.49.own_ref, ...), custom_call_target="tpu_custom_call" | custom-call | flops 12000000000 | bytes 8388608 | tf_op jit(solution)/shard_map/attention_forward/pallas_call | solution.py:266
  93.8 1.7 collective-permute-done.31.rest_12_
  98.4 22.8 %feed_forward.2 = (bf16[4,512,768]{2,1,0:T(8,128)(2,1)}, bf16[1,512,768]{2,1,0:T(8,128)(2,1)}, f32[1,512,768]{2,1,0:T(8,128)}, bf16[1,512,768]{2,1,0:T(8,128)(2,1)}) custom-call(s32[10]{0:T(128)} %get-tuple-element.51.info, bf16[4,512,768]{2,1,0:T(8,128)(2,1)} %x_ref.7, bf16[1,512,768]{2,1,0:T(8,128)(2,1)} %get-tuple-element.53.ctx_ref, ...), custom_call_target="tpu_custom_call" | custom-call | flops 24000000000 | bytes 8388608 | tf_op jit(solution)/shard_map/feed_forward/pallas_call | solution.py:401
  122.0 17.6 %attention_backward.2 = (bf16[4,512,768]{2,1,0:T(8,128)(2,1)}, bf16[1,512,768]{2,1,0:T(8,128)(2,1)}, f32[8,768]{1,0:T(8,128)}, f32[8,768]{1,0:T(8,128)}) custom-call(s32[10]{0:T(128)} %get-tuple-element.51.info, bf16[2,512,1152]{2,1,0:T(8,128)(2,1)} %get-tuple-element.67.qkv_ref, bf16[2,6,512,512]{3,2,1,0:T(8,128)(2,1)} %get-tuple-element.68.p_ref, ...), custom_call_target="tpu_custom_call" | custom-call | flops 16000000000 | bytes 8388608 | tf_op jit(solution)/shard_map/attention_backward/pallas_call | solution.py:534
  141.1 22.6 %feed_forward.3 = (bf16[4,512,768]{2,1,0:T(8,128)(2,1)}, bf16[1,512,768]{2,1,0:T(8,128)(2,1)}, f32[1,512,768]{2,1,0:T(8,128)}, bf16[1,512,768]{2,1,0:T(8,128)(2,1)}) custom-call(s32[10]{0:T(128)} %get-tuple-element.51.info, bf16[4,512,768]{2,1,0:T(8,128)(2,1)} %x_ref.7, ...), custom_call_target="tpu_custom_call", output_to_operand_aliasing={{0}: (24, {})} | custom-call | flops 24000000000 | bytes 8388608 | tf_op jit(solution)/shard_map/feed_forward/pallas_call | solution.py:401
  164.7 15.3 %attention_backward.3 = (bf16[4,512,768]{2,1,0:T(8,128)(2,1)}, bf16[1,512,768]{2,1,0:T(8,128)(2,1)}, f32[8,768]{1,0:T(8,128)}, f32[8,768]{1,0:T(8,128)}) custom-call(s32[10]{0:T(128)} %get-tuple-element.51.info, bf16[2,512,1152]{2,1,0:T(8,128)(2,1)} %get-tuple-element.77.qkv_ref, ...), custom_call_target="tpu_custom_call", output_to_operand_aliasing={{0}: (28, {})} | custom-call | flops 16000000000 | bytes 8388608 | tf_op jit(solution)/shard_map/attention_backward/pallas_call | solution.py:534
  181.1 2.9 %collective-permute-done.38 = f32[8,768]{1,0:T(8,128)S(1)} collective-permute-done((f32[8,768]{1,0:T(8,128)}, f32[8,768]{1,0:T(8,128)S(1)}, u32[]{:S(2)}, u32[]{:S(2)}) %collective-permute-start.38) | collective-permute-done | bytes 24608 | tf_op jit(solution)/shard_map/ppermute | solution.py:667
  188.1 2.9 %collective-permute-done.41 = f32[8,768]{1,0:T(8,128)S(1)} collective-permute-done((f32[8,768]{1,0:T(8,128)S(1)}, f32[8,768]{1,0:T(8,128)S(1)}, u32[]{:S(2)}, u32[]{:S(2)}) %collective-permute-start.41) | collective-permute-done | bytes 24608 | tf_op jit(solution)/shard_map/ppermute | solution.py:602
  190.9 1.6 collective-permute-start.42
  192.6 2.2 %collective-permute-done.42 = f32[8,768]{1,0:T(8,128)S(1)} collective-permute-done((f32[8,768]{1,0:T(8,128)S(1)}, f32[8,768]{1,0:T(8,128)S(1)}, u32[]{:S(2)}, u32[]{:S(2)}) %collective-permute-start.42) | collective-permute-done | bytes 24608 | tf_op jit(solution)/shard_map/ppermute | solution.py:602
  194.8 4.7 %collective-permute-start.43 = (f32[8,768]{1,0:T(8,128)S(1)}, f32[8,768]{1,0:T(8,128)S(1)}, u32[]{:S(2)}, u32[]{:S(2)}) collective-permute-start(f32[8,768]{1,0:T(8,128)S(1)} %add.18), channel_id=1, source_target_pairs={{0,16},{2,18},{4,20},{6,22},{8,24},{10,26},{12,28},{14,30},{16,0},... | collective-permute-start | bytes 73736 | tf_op jit(solution)/shard_map/ppermute | solution.py:602
  201.9 1.7 place.3
  (142 shorter events, 38.8 us)
Async XLA Ops:
  2.1 8.3 %collective-permute-start.1 = (bf16[48,1152]{1,0:T(8,128)(2,1)}, bf16[48,1152]{1,0:T(8,128)(2,1)S(1)}, u32[]{:S(2)}, u32[]{:S(2)}) collective-permute-start(bf16[48,1152]{1,0:T(8,128)(2,1)} %pack.1), channel_id=1, source_target_pairs={{0,8},{1,9},{2,10},{3,11},{4,12},{5,13},{6,14},{7,15},{8,16},{9,17... | collective-permute-start | bytes 331784 | tf_op jit(solution)/shard_map/ppermute | solution.py:54
  12.3 15.6 %collective-permute-start.18 = (bf16[48,3456]{1,0:T(8,128)(2,1)}, bf16[48,3456]{1,0:T(8,128)(2,1)S(1)}, u32[]{:S(2)}, u32[]{:S(2)}) collective-permute-start(bf16[48,3456]{1,0:T(8,128)(2,1)} %get-tuple-element.56), channel_id=1, source_target_pairs={{0,8},{1,9},{2,10},{3,11},{4,12},{5,13},{6,14},{7,15},{8,16},{9,17... | collective-permute-start | bytes 995336 | tf_op jit(solution)/shard_map/ppermute | solution.py:54
  13.7 14.3 %collective-permute-start = (f32[22,384]{1,0:T(8,128)}, f32[22,384]{1,0:T(8,128)S(1)}, u32[]{:S(2)}, u32[]{:S(2)}) collective-permute-start(f32[22,384]{1,0:T(8,128)} %get-tuple-element.49.own_ref), channel_id=1, source_target_pairs={{0,1},{1,0},{2,3},{3,2},{4,5},{5,4},{6,7},{7,6},{8,9},{9,8},{10,11... | collective-permute-start | bytes 101384 | tf_op jit(solution)/shard_map/ppermute | solution.py:624
  17.7 8.7 %collective-permute-start.10 = (bf16[48,1152]{1,0:T(8,128)(2,1)S(1)}, bf16[48,1152]{1,0:T(8,128)(2,1)S(1)}, u32[]{:S(2)}, u32[]{:S(2)}) collective-permute-start(bf16[48,1152]{1,0:T(8,128)(2,1)S(1)} %collective-permute-done.9), channel_id=1, source_target_pairs={{0,8},{1,9},{2,10},{3,11},{4,12},{5,13},{6,14},{7,15},{8,16},{9,17... | collective-permute-start | bytes 331784 | tf_op jit(solution)/shard_map/ppermute | solution.py:54
  17.8 10.3 %collective-permute-start.5 = (bf16[2,48,1152]{2,1,0:T(8,128)(2,1)S(1)}, bf16[2,48,1152]{2,1,0:T(8,128)(2,1)S(1)}, u32[]{:S(2)}, u32[]{:S(2)}) collective-permute-start(bf16[2,48,1152]{2,1,0:T(8,128)(2,1)S(1)} %pad_maximum_fusion.2.rest_0_), channel_id=1, source_target_pairs={{0,2},{1,3},{2,0},{3,1},{4,6},{5,7},{6,4},{7,5},{8,10},{9,11},{10,... | collective-permute-start | bytes 663560 | tf_op jit(solution)/shard_map/ppermute | solution.py:54
  17.9 11.8 %collective-permute-start.3 = (bf16[2,48,1152]{2,1,0:T(8,128)(2,1)S(1)}, bf16[2,48,1152]{2,1,0:T(8,128)(2,1)S(1)}, u32[]{:S(2)}, u32[]{:S(2)}) collective-permute-start(bf16[2,48,1152]{2,1,0:T(8,128)(2,1)S(1)} %pad_maximum_fusion.2.rest_0_), channel_id=1, source_target_pairs={{0,1},{1,0},{2,6},{3,7},{4,5},{5,4},{6,2},{7,3},{8,9},{9,8},{10,14... | collective-permute-start | bytes 663560 | tf_op jit(solution)/shard_map/ppermute | solution.py:54
  27.9 10.7 %collective-permute-start.26 = (bf16[48,3456]{1,0:T(8,128)(2,1)S(1)}, bf16[48,3456]{1,0:T(8,128)(2,1)S(1)}, u32[]{:S(2)}, u32[]{:S(2)}) collective-permute-start(bf16[48,3456]{1,0:T(8,128)(2,1)S(1)} %collective-permute-done.18), channel_id=1, source_target_pairs={{0,8},{1,9},{2,10},{3,11},{4,12},{5,13},{6,14},{7,15},{8,16},{9,17... | collective-permute-start | bytes 995336 | tf_op jit(solution)/shard_map/ppermute | solution.py:54
  38.6 11.1 %collective-permute-start.27 = (bf16[48,3456]{1,0:T(8,128)(2,1)S(1)}, bf16[48,3456]{1,0:T(8,128)(2,1)S(1)}, u32[]{:S(2)}, u32[]{:S(2)}) collective-permute-start(bf16[48,3456]{1,0:T(8,128)(2,1)S(1)} %collective-permute-done.26), channel_id=1, source_target_pairs={{0,8},{1,9},{2,10},{3,11},{4,12},{5,13},{6,14},{7,15},{8,16},{9,17... | collective-permute-start | bytes 995336 | tf_op jit(solution)/shard_map/ppermute | solution.py:54
  39.7 12.3 %collective-permute-start.19 = (bf16[2,48,3456]{2,1,0:T(8,128)(2,1)S(1)}, bf16[2,48,3456]{2,1,0:T(8,128)(2,1)S(1)}, u32[]{:S(2)}, u32[]{:S(2)}) collective-permute-start(bf16[2,48,3456]{2,1,0:T(8,128)(2,1)S(1)} %pad_maximum_fusion.rest_0_), channel_id=1, source_target_pairs={{0,4},{1,5},{2,3},{3,2},{4,0},{5,1},{6,7},{7,6},{8,12},{9,13},{10,... | collective-permute-start | bytes 1990664 | tf_op jit(solution)/shard_map/ppermute | solution.py:54
  40.9 9.0 %collective-permute-start.16 = (bf16[2,48,1152]{2,1,0:T(8,128)(2,1)S(1)}, bf16[2,48,1152]{2,1,0:T(8,128)(2,1)S(1)}, u32[]{:S(2)}, u32[]{:S(2)}) collective-permute-start(bf16[2,48,1152]{2,1,0:T(8,128)(2,1)S(1)} %collective-permute-done.12.rest_10_), channel_id=1, source_target_pairs={{0,2},{1,3},{2,0},{3,1},{4,6},{5,7},{6,4},{7,5},{8,10},{9,11},{10,... | collective-permute-start | bytes 663560 | tf_op jit(solution)/shard_map/ppermute | solution.py:54
  40.9 9.5 %collective-permute-start.15 = (bf16[2,48,1152]{2,1,0:T(8,128)(2,1)S(1)}, bf16[2,48,1152]{2,1,0:T(8,128)(2,1)S(1)}, u32[]{:S(2)}, u32[]{:S(2)}) collective-permute-start(bf16[2,48,1152]{2,1,0:T(8,128)(2,1)S(1)} %collective-permute-done.11.rest_9_), channel_id=1, source_target_pairs={{0,2},{1,3},{2,0},{3,1},{4,6},{5,7},{6,4},{7,5},{8,10},{9,11},{10,... | collective-permute-start | bytes 663560 | tf_op jit(solution)/shard_map/ppermute | solution.py:54
  43.0 9.5 %collective-permute-start.8 = (bf16[2,48,1152]{2,1,0:T(8,128)(2,1)S(1)}, bf16[2,48,1152]{2,1,0:T(8,128)(2,1)S(1)}, u32[]{:S(2)}, u32[]{:S(2)}) collective-permute-start(bf16[2,48,1152]{2,1,0:T(8,128)(2,1)S(1)} %collective-permute-done.4.rest_3_), channel_id=1, source_target_pairs={{0,2},{1,3},{2,0},{3,1},{4,6},{5,7},{6,4},{7,5},{8,10},{9,11},{10,... | collective-permute-start | bytes 663560 | tf_op jit(solution)/shard_map/ppermute | solution.py:54
  49.9 23.7 %collective-permute-start.20 = (bf16[2,48,3456]{2,1,0:T(8,128)(2,1)S(1)}, bf16[2,48,3456]{2,1,0:T(8,128)(2,1)S(1)}, u32[]{:S(2)}, u32[]{:S(2)}) collective-permute-start(bf16[2,48,3456]{2,1,0:T(8,128)(2,1)S(1)} %pad_maximum_fusion.rest_0_), channel_id=1, source_target_pairs={{0,1},{1,0},{2,6},{3,7},{4,5},{5,4},{6,2},{7,3},{8,9},{9,8},{10,14... | collective-permute-start | bytes 1990664 | tf_op jit(solution)/shard_map/ppermute | solution.py:54
  50.4 23.1 %collective-permute-start.29 = (bf16[2,48,3456]{2,1,0:T(8,128)(2,1)S(1)}, bf16[2,48,3456]{2,1,0:T(8,128)(2,1)}, u32[]{:S(2)}, u32[]{:S(2)}) collective-permute-start(bf16[2,48,3456]{2,1,0:T(8,128)(2,1)S(1)} %pad_maximum_fusion.1.rest_8_), channel_id=1, source_target_pairs={{0,1},{1,0},{2,6},{3,7},{4,5},{5,4},{6,2},{7,3},{8,9},{9,8},{10,14... | collective-permute-start | bytes 1990664 | tf_op jit(solution)/shard_map/ppermute | solution.py:54
  52.0 23.0 %collective-permute-start.21 = (bf16[2,48,3456]{2,1,0:T(8,128)(2,1)S(1)}, bf16[2,48,3456]{2,1,0:T(8,128)(2,1)}, u32[]{:S(2)}, u32[]{:S(2)}) collective-permute-start(bf16[2,48,3456]{2,1,0:T(8,128)(2,1)S(1)} %collective-permute-done.19.rest_1_), channel_id=1, source_target_pairs={{0,1},{1,0},{2,6},{3,7},{4,5},{5,4},{6,2},{7,3},{8,9},{9,8},{10,14... | collective-permute-start | bytes 1990664 | tf_op jit(solution)/shard_map/ppermute | solution.py:54
  72.3 19.1 %collective-permute-start.28 = (bf16[2,48,3456]{2,1,0:T(8,128)(2,1)S(1)}, bf16[2,48,3456]{2,1,0:T(8,128)(2,1)}, u32[]{:S(2)}, u32[]{:S(2)}) collective-permute-start(bf16[2,48,3456]{2,1,0:T(8,128)(2,1)S(1)} %pad_maximum_fusion.1.rest_8_), channel_id=1, source_target_pairs={{0,4},{1,5},{2,3},{3,2},{4,0},{5,1},{6,7},{7,6},{8,12},{9,13},{10,... | collective-permute-start | bytes 1990664 | tf_op jit(solution)/shard_map/ppermute | solution.py:54
  74.9 17.1 %collective-permute-start.22 = (bf16[2,48,3456]{2,1,0:T(8,128)(2,1)S(1)}, bf16[2,48,3456]{2,1,0:T(8,128)(2,1)}, u32[]{:S(2)}, u32[]{:S(2)}) collective-permute-start(bf16[2,48,3456]{2,1,0:T(8,128)(2,1)S(1)} %pad_maximum_fusion.rest_0_), channel_id=1, source_target_pairs={{0,2},{1,3},{2,0},{3,1},{4,6},{5,7},{6,4},{7,5},{8,10},{9,11},{10,... | collective-permute-start | bytes 1990664 | tf_op jit(solution)/shard_map/ppermute | solution.py:54
  74.9 17.2 %collective-permute-start.23 = (bf16[2,48,3456]{2,1,0:T(8,128)(2,1)S(1)}, bf16[2,48,3456]{2,1,0:T(8,128)(2,1)}, u32[]{:S(2)}, u32[]{:S(2)}) collective-permute-start(bf16[2,48,3456]{2,1,0:T(8,128)(2,1)S(1)} %collective-permute-done.19.rest_1_), channel_id=1, source_target_pairs={{0,2},{1,3},{2,0},{3,1},{4,6},{5,7},{6,4},{7,5},{8,10},{9,11},{10,... | collective-permute-start | bytes 1990664 | tf_op jit(solution)/shard_map/ppermute | solution.py:54
  75.4 17.1 %collective-permute-start.24 = (bf16[2,48,3456]{2,1,0:T(8,128)(2,1)S(1)}, bf16[2,48,3456]{2,1,0:T(8,128)(2,1)}, u32[]{:S(2)}, u32[]{:S(2)}) collective-permute-start(bf16[2,48,3456]{2,1,0:T(8,128)(2,1)S(1)} %collective-permute-done.20.rest_2_), channel_id=1, source_target_pairs={{0,2},{1,3},{2,0},{3,1},{4,6},{5,7},{6,4},{7,5},{8,10},{9,11},{10,... | collective-permute-start | bytes 1990664 | tf_op jit(solution)/shard_map/ppermute | solution.py:54
  75.5 16.0 %collective-permute-start.30 = (bf16[2,48,3456]{2,1,0:T(8,128)(2,1)}, bf16[2,48,3456]{2,1,0:T(8,128)(2,1)}, u32[]{:S(2)}, u32[]{:S(2)}) collective-permute-start(bf16[2,48,3456]{2,1,0:T(8,128)(2,1)} %collective-permute-done.29.rest_10_), channel_id=1, source_target_pairs={{0,4},{1,5},{2,3},{3,2},{4,0},{5,1},{6,7},{7,6},{8,12},{9,13},{10,... | collective-permute-start | bytes 1990664 | tf_op jit(solution)/shard_map/ppermute | solution.py:54
  121.2 19.9 %collective-permute-start.35 = (bf16[1,512,768]{2,1,0:T(8,128)(2,1)}, bf16[1,512,768]{2,1,0:T(8,128)(2,1)S(1)}, u32[]{:S(2)}, u32[]{:S(2)}) collective-permute-start(bf16[1,512,768]{2,1,0:T(8,128)(2,1)} %get-tuple-element.66), channel_id=1, source_target_pairs={{0,1},{1,0},{2,3},{3,2},{4,5},{5,4},{6,7},{7,6},{8,9},{9,8},{10,11... | collective-permute-start | bytes 2359304 | tf_op jit(solution)/shard_map/ppermute | solution.py:659
  139.6 25.0 %collective-permute-start.37 = (bf16[1,512,768]{2,1,0:T(8,128)(2,1)}, bf16[1,512,768]{2,1,0:T(8,128)(2,1)S(1)}, u32[]{:S(2)}, u32[]{:S(2)}) collective-permute-start(bf16[1,512,768]{2,1,0:T(8,128)(2,1)} %get-tuple-element.72), channel_id=1, source_target_pairs={{0,1},{1,0},{2,3},{3,2},{4,5},{5,4},{6,7},{7,6},{8,9},{9,8},{10,11... | collective-permute-start | bytes 2359304 | tf_op jit(solution)/shard_map/ppermute | solution.py:661
  163.6 20.4 %collective-permute-start.36 = (bf16[1,512,768]{2,1,0:T(8,128)(2,1)}, bf16[1,512,768]{2,1,0:T(8,128)(2,1)S(1)}, u32[]{:S(2)}, u32[]{:S(2)}) collective-permute-start(bf16[1,512,768]{2,1,0:T(8,128)(2,1)} %get-tuple-element.76), channel_id=1, source_target_pairs={{0,1},{1,0},{2,3},{3,2},{4,5},{5,4},{6,7},{7,6},{8,9},{9,8},{10,11... | collective-permute-start | bytes 2359304 | tf_op jit(solution)/shard_map/ppermute | solution.py:664
  184.1 19.5 %collective-permute-start.39 = (bf16[1,512,768]{2,1,0:T(8,128)(2,1)}, bf16[1,512,768]{2,1,0:T(8,128)(2,1)S(1)}, u32[]{:S(2)}, u32[]{:S(2)}) collective-permute-start(bf16[1,512,768]{2,1,0:T(8,128)(2,1)} %get-tuple-element.89), channel_id=1, source_target_pairs={{0,1},{1,0},{2,3},{3,2},{4,5},{5,4},{6,7},{7,6},{8,9},{9,8},{10,11... | collective-permute-start | bytes 2359304 | tf_op jit(solution)/shard_map/ppermute | solution.py:668
  (48 other events, 513.2 us)
